TPU v7x, 32 devices: a whole 2x2x4 slice. The times are simulated.
32 devices in a mesh: dp: 16 (over z, x, core), head: 2 (over y).
Axes of the slice: x: 2, y: 2, z: 4, core: 2. Of those that a mesh axis runs over, the one named last changes fastest.
Arguments:
- x_input: bfloat16 [2048, 8192], P('dp'), may hold values from -8 to 8
- wq_old: bfloat16 [8192, 1024], P('dp', 'head'), may hold values from -0.0625 to 0.0625
- wq_fresh: bfloat16 [8192, 256], P('dp', 'head'), may hold values from -0.0625 to 0.0625
- key_projection_weight: bfloat16 [8192, 256], P('dp', 'head'), may hold values from -0.0625 to 0.0625
- value_projection_weight: bfloat16 [8192, 256], P('dp', 'head'), may hold values from -0.0625 to 0.0625
- attention_output_gradient: bfloat16 [2048, 1280], P('dp', 'head'), may hold values from -6 to 6
- head_source: int32 [10], replicated, may hold values from 0 to 9, as said below
- doc_ids: int32 [2048], P('dp'), may hold values from 0 to 63, never falling along the last dimension, each value on 1 to 128 neighbouring positions
Outputs:
- attn_out: bfloat16 [2048, 1280], P('dp', 'head')
- x_grad: bfloat16 [2048, 8192], P('dp', 'head')
Inputs may be any that keep to these rules, and one draw needn't show every extreme that they name: head_source is a permutation. There are shifts s_k and a permutation t of the 5 local indices, the same for every owner d, such that new head d * 5 + k takes candidate ((d - s_k) mod 2) * 5 + t_k; one owner takes at most 3 new head from any one former owner, and some pair reaches 3.
All inputs are finite; a program needn't handle non-finite values.
Results may differ from a plain program's by a relative error of at most 0.014.
The roundings to bfloat16 on the way count: a program that leaves them out, or rounds other values in their place, can miss the bound.
Values may be sent and summed in bfloat16 or wider, within the bound.
A program may use at most 64 MiB of HBM per device.

v0:
```python
import functools
import math

import jax
import jax.numpy as jnp
import numpy as np
from jax import lax
from jax.experimental import pallas as pl
from jax.experimental.pallas import tpu as pltpu
from jax.sharding import PartitionSpec as P

theta_base = 500000.0
neg_large = -1e30
MESH = pl.DeviceIdType.MESH


def rotary_tables(length, width):
    half = width // 2
    frequency = theta_base ** (-2.0 * np.arange(half, dtype=np.float64) / width)
    angles = np.arange(length, dtype=np.float64)[:, None] * frequency[None, :]
    cosine, sine = np.cos(angles), np.sin(angles)
    return (
        np.concatenate([cosine, cosine], axis=1).astype(np.float32),
        np.concatenate([-sine, sine], axis=1).astype(np.float32),
    )


def dot(a, b, ca, cb):
    return lax.dot_general(
        a, b, (((ca,), (cb,)), ((), ())), preferred_element_type=jnp.float32
    )


def kernel(
    n_dp, n_head, group, ways,
    src_ref, doc_hbm, cos_hbm, sin_hbm, x_hbm, old_hbm, fresh_hbm, k_hbm, v_hbm, g_hbm,
    out_ref, grad_ref,
    doc_ref, cos_ref, sin_ref, x_ref, own_ref, g_ref, wq, wkv, parcel, arrived, accq, acckv, dq_ref, dkv_ref,
    psend, precv,
    in_sem, rs, rr, cs, cr, hs, hr, ps, pr,
):
    me, head = lax.axis_index("dp"), lax.axis_index("head")
    rows, hd = k_hbm.shape
    length = x_ref.shape[0]
    lanes = 2
    m = n_dp // lanes
    core, chip = me % lanes, me // lanes
    side, level = chip % 2, chip // 2
    pos = (1 - side) * level + side * (m - 1 - level)
    piece = rows // ways
    sub = piece // 2
    lead = min(2, m - 2)
    parts = 3
    capacity = parcel.shape[2]
    signs = (1, -1)[:ways]
    bufs = (wkv, wq)
    spans = ((0, piece), (0, sub), (sub, sub))

    def index_of(p, lane):
        p = (p + 2 * m) % m
        far = p // (m // 2)
        return ((1 - far) * 2 * p + far * (2 * (m - 1 - p) + 1)) * lanes + lane

    right, left = index_of(pos + 1, core), index_of(pos - 1, core)
    targets = (right, left)[:ways]
    partner = index_of(pos, 1 - core)

    loads = [
        pltpu.make_async_copy(k_hbm, wkv.at[me, :, pl.ds(0, hd)], in_sem.at[0]),
        pltpu.make_async_copy(v_hbm, wkv.at[me, :, pl.ds(hd, hd)], in_sem.at[1]),
        pltpu.make_async_copy(old_hbm, own_ref.at[:, pl.ds(0, (group - 1) * hd)], in_sem.at[2]),
        pltpu.make_async_copy(fresh_hbm, own_ref.at[:, pl.ds((group - 1) * hd, hd)], in_sem.at[3]),
        pltpu.make_async_copy(x_hbm, x_ref, in_sem.at[4]),
        pltpu.make_async_copy(g_hbm, g_ref, in_sem.at[5]),
        pltpu.make_async_copy(doc_hbm, doc_ref, in_sem.at[6]),
        pltpu.make_async_copy(cos_hbm, cos_ref, in_sem.at[7]),
        pltpu.make_async_copy(sin_hbm, sin_ref, in_sem.at[8]),
    ]
    for load in loads:
        load.start()

    barrier = pltpu.get_barrier_semaphore()
    peers = [(right, head), (left, head), (partner, head)]
    peers += [(me, (head + j) % n_head) for j in range(1, n_head)]
    for peer in peers:
        pl.semaphore_signal(barrier, inc=1, device_id=peer, device_id_type=MESH)

    def part_of(p, w, owner):
        first, count = spans[p]
        return bufs[min(p, 1)].at[owner, pl.ds(w * piece + first, count)]

    def ring(p, w, s):
        ref = part_of(p, w, index_of(pos - signs[w] * s, core))
        return pltpu.make_async_remote_copy(
            ref, ref, rs.at[w * parts + p, s], rr.at[w * parts + p, s],
            device_id=(targets[w], head), device_id_type=MESH)

    def ring_in(p, w, s):
        ref = part_of(p, w, index_of(pos - signs[w] * (s + 1), core))
        return pltpu.make_async_remote_copy(
            ref, ref, rs.at[w * parts + p, s], rr.at[w * parts + p, s],
            device_id=(targets[w], head), device_id_type=MESH)

    def across(p, w, s, lane):
        ref = part_of(p, w, index_of(pos - signs[w] * s, lane))
        return pltpu.make_async_remote_copy(
            ref, ref, cs.at[w * parts + p, s], cr.at[w * parts + p, s],
            device_id=(partner, head), device_id_type=MESH)

    def relay(u, j):
        return pltpu.make_async_remote_copy(
            parcel.at[u, j - 1], arrived.at[u, j - 1], hs.at[u, j - 1], hr.at[u, j - 1],
            device_id=(me, (head + j) % n_head), device_id_type=MESH)

    shift = [(n_head - src_ref[k] // group) % n_head for k in range(group)]
    taken = [src_ref[k] % group for k in range(group)]
    slot = [
        sum([(shift[l] == shift[k]).astype(jnp.int32) for l in range(k)], jnp.int32(0))
        for k in range(group)
    ]

    def flag(cond):
        return jnp.where(cond, 1.0, 0.0).astype(jnp.float32)

    units = [w * 2 + half for half in range(2) for w in range(ways)]

    def weigh(u, weights):
        total = jnp.zeros((sub, hd), jnp.float32)
        for c_m in range(group):
            block = own_ref[u * sub:(u + 1) * sub, c_m * hd:(c_m + 1) * hd]
            total = total + block.astype(jnp.float32) * weights[c_m]
        return total.astype(jnp.bfloat16)

    for load in loads[:2]:
        load.wait()
    pl.semaphore_wait(barrier, len(peers))
    for w in range(ways):
        ring(0, w, 0).start()
    for w in range(ways):
        across(0, w, 0, core).start()
    for load in loads[2:4]:
        load.wait()
    for u in units:
        for j in range(1, n_head):
            for c in range(capacity):
                weights = [
                    sum([flag((shift[k] == j) & (slot[k] == c) & (taken[k] == c_m))
                         for k in range(group)], jnp.float32(0))
                    for c_m in range(group)
                ]
                parcel[u, j - 1, c] = weigh(u, weights)
            relay(u, j).start()
    for k in range(group):
        weights = [flag((shift[k] == 0) & (taken[k] == c_m)) for c_m in range(group)]
        for u in units:
            wq[me, u * sub:(u + 1) * sub, k * hd:(k + 1) * hd] = weigh(u, weights)
    for load in loads[4:]:
        load.wait()
    accq[...] = jnp.zeros_like(accq)
    acckv[...] = jnp.zeros_like(acckv)

    def add(p, w, owner):
        xs = x_ref[:, pl.ds(pl.multiple_of(owner * rows + w * piece, 128), piece)]
        acc = (acckv, accq)[p]
        acc[...] += dot(xs, bufs[p][owner, pl.ds(w * piece, piece), :], 1, 0)

    def pass_on(p, w, s):
        ring_in(p, w, s - 1).wait_recv()

        @pl.when(s < m - 1)
        def _():
            ring(p, w, s).start()

        across(p, w, s, core).start()

    def unit_out(u):
        block = pl.ds(u * sub, sub)
        for j in range(1, n_head):
            relay(u, j).wait_recv()
        for k in range(group):
            cols = slice(k * hd, (k + 1) * hd)
            total = wq[me, block, cols].astype(jnp.float32)
            for j in range(1, n_head):
                for c in range(capacity):
                    weight = flag((shift[k] == j) & (slot[k] == c))
                    total = total + arrived[u, j - 1, c].astype(jnp.float32) * weight
            wq[me, block, cols] = total.astype(jnp.bfloat16)
        ring(1 + u % 2, u // 2, 0).start()
        across(1 + u % 2, u // 2, 0, core).start()

    for w in range(ways):
        add(0, w, me)
    for u in units[:ways]:
        unit_out(u)
    for s in range(1, lead + 1):
        for w in range(ways):
            pass_on(0, w, s)
        if s == 1:
            for u in units[ways:]:
                unit_out(u)
    for w in range(ways):
        add(1, w, me)

    def step(s, carry):
        @pl.when(s + lead < m)
        def _():
            for w in range(ways):
                pass_on(0, w, s + lead)

        for p in range(1, parts):
            for w in range(ways):
                pass_on(p, w, s)
        for w in range(ways):
            for p in range(2):
                add(p, w, index_of(pos - signs[w] * s, core))
        for w in range(ways):
            for p in range(parts):
                across(p, w, s - 1, 1 - core).wait_recv()
        for w in range(ways):
            for p in range(2):
                add(p, w, index_of(pos - signs[w] * (s - 1), 1 - core))
        return carry

    lax.fori_loop(1, m, step, 0)
    for w in range(ways):
        for p in range(parts):
            across(p, w, m - 1, 1 - core).wait_recv()
        for p in range(2):
            add(p, w, index_of(pos - signs[w] * (m - 1), 1 - core))

    scale = 1.0 / math.sqrt(hd)
    cosine, sine = cos_ref[...], sin_ref[...]

    def rotate(f):
        return f * cosine + pltpu.roll(f, hd // 2, 1) * sine

    def rotate_back(f):
        return f * cosine - pltpu.roll(f, hd // 2, 1) * sine

    docs = jnp.broadcast_to(doc_ref[...].astype(jnp.float32), (length, length))
    at_key = lax.broadcasted_iota(jnp.int32, (length, length), 1)
    at_query = lax.broadcasted_iota(jnp.int32, (length, length), 0)
    allowed = (at_key <= at_query) & (docs == docs.T)
    key = rotate(acckv[:, :hd]).astype(jnp.bfloat16)
    value = acckv[:, hd:].astype(jnp.bfloat16)
    dkey = jnp.zeros((length, hd), jnp.float32)
    dvalue = jnp.zeros((length, hd), jnp.float32)
    for k in range(group):
        cols = slice(k * hd, (k + 1) * hd)
        query = rotate(accq[:, cols]).astype(jnp.bfloat16)
        given = g_ref[:, cols]
        scores = jnp.where(allowed, dot(query, key, 1, 1) * scale, neg_large)
        weights = jnp.exp(scores - jnp.max(scores, axis=-1, keepdims=True))
        probs = weights / jnp.sum(weights, axis=-1, keepdims=True)
        probs_b = probs.astype(jnp.bfloat16)
        out_ref[:, cols] = dot(probs_b, value, 1, 0).astype(jnp.bfloat16)
        prob_grad = dot(given, value, 1, 1)
        centre = jnp.sum(probs * prob_grad, axis=-1, keepdims=True)
        dscore = (probs * (prob_grad - centre) * scale).astype(jnp.bfloat16)
        dq_ref[:, cols] = rotate_back(dot(dscore, key, 1, 0)).astype(jnp.bfloat16)
        dkey = dkey + dot(dscore, query, 0, 0)
        dvalue = dvalue + dot(probs_b, given, 0, 0)
    dkv_ref[:, :hd] = rotate_back(dkey).astype(jnp.bfloat16)
    dkv_ref[:, hd:] = dvalue.astype(jnp.bfloat16)

    chunks = n_dp // n_head

    def partial(owner):
        return (dot(dq_ref[...], wq[owner], 1, 1) + dot(dkv_ref[...], wkv[owner], 1, 1)).astype(
            jnp.bfloat16)

    def share(j, i):
        return pltpu.make_async_remote_copy(
            psend.at[j - 1, i], precv.at[j - 1, i], ps.at[j - 1, i], pr.at[j - 1, i],
            device_id=(me, (head + j) % n_head), device_id_type=MESH)

    for j in range(1, n_head):
        def send_chunk(i, carry):
            psend[j - 1, i] = partial(((head + j) % n_head) * chunks + i)
            share(j, i).start()
            return carry

        lax.fori_loop(0, chunks, send_chunk, 0)

    def own_chunk(i, carry):
        cols = pl.ds(pl.multiple_of(i * rows, 128), rows)
        grad_ref[:, cols] = partial(head * chunks + i)
        return carry

    lax.fori_loop(0, chunks, own_chunk, 0)

    def finish(i, carry):
        cols = pl.ds(pl.multiple_of(i * rows, 128), rows)
        total = grad_ref[:, cols].astype(jnp.float32)
        for j in range(1, n_head):
            share(j, i).wait_recv()
            total = total + precv[j - 1, i].astype(jnp.float32)
        grad_ref[:, cols] = total.astype(jnp.bfloat16)
        return carry

    lax.fori_loop(0, chunks, finish, 0)

    def drain(s, carry):
        for p in range(parts):
            for w in range(ways):
                @pl.when(s < m - 1)
                def _():
                    ring(p, w, s).wait_send()

                across(p, w, s, core).wait_send()
        return carry

    lax.fori_loop(0, m, drain, 0)
    for j in range(1, n_head):
        for u in units:
            relay(u, j).wait_send()

        def drain_share(i, carry):
            share(j, i).wait_send()
            return carry

        lax.fori_loop(0, chunks, drain_share, 0)


def solution(mesh):
    n_dp, n_head = mesh.shape["dp"], mesh.shape["head"]

    def local(x, old, fresh, wk, wv, g, head_source, doc_ids):
        length, width = x.shape
        rows, hd = wk.shape
        group = g.shape[1] // hd
        ways = 2 if rows % 256 == 0 else 1
        m = n_dp // 2
        capacity = (group + n_head - 1) // n_head
        chunks = n_dp // n_head
        cosine, sine = rotary_tables(length, hd)
        bf, f32 = jnp.bfloat16, jnp.float32
        vm = pl.BlockSpec(memory_space=pltpu.VMEM)
        anyspace = pl.BlockSpec(memory_space=pl.ANY)
        dma = pltpu.SemaphoreType.DMA
        return pl.pallas_call(
            functools.partial(kernel, n_dp, n_head, group, ways),
            out_shape=(
                jax.ShapeDtypeStruct((length, group * hd), bf),
                jax.ShapeDtypeStruct((length, width // n_head), bf),
            ),
            in_specs=[pl.BlockSpec(memory_space=pltpu.SMEM)] + [anyspace] * 9,
            out_specs=(vm, vm),
            scratch_shapes=[
                pltpu.VMEM((1, length), jnp.int32),
                pltpu.VMEM((length, hd), f32),
                pltpu.VMEM((length, hd), f32),
                pltpu.VMEM((length, width), bf),
                pltpu.VMEM((rows, group * hd), bf),
                pltpu.VMEM((length, group * hd), bf),
                pltpu.VMEM((n_dp, rows, group * hd), bf),
                pltpu.VMEM((n_dp, rows, 2 * hd), bf),
                pltpu.VMEM((2 * ways, n_head - 1, capacity, rows // (2 * ways), hd), bf),
                pltpu.VMEM((2 * ways, n_head - 1, capacity, rows // (2 * ways), hd), bf),
                pltpu.VMEM((length, group * hd), f32),
                pltpu.VMEM((length, 2 * hd), f32),
                pltpu.VMEM((length, group * hd), bf),
                pltpu.VMEM((length, 2 * hd), bf),
                pltpu.VMEM((n_head - 1, chunks, length, rows), bf),
                pltpu.VMEM((n_head - 1, chunks, length, rows), bf),
                dma((9,)),
                dma((3 * ways, m)),
                dma((3 * ways, m)),
                dma((3 * ways, m)),
                dma((3 * ways, m)),
                dma((2 * ways, n_head - 1)),
                dma((2 * ways, n_head - 1)),
                dma((n_head - 1, chunks)),
                dma((n_head - 1, chunks)),
            ],
            compiler_params=pltpu.CompilerParams(
                collective_id=0, has_side_effects=True, vmem_limit_bytes=67043328),
        )(head_source, doc_ids.reshape(1, -1), cosine, sine, x, old, fresh, wk, wv, g)

    in_specs = (
        P("dp", None), P("dp", "head"), P("dp", "head"), P("dp", "head"),
        P("dp", "head"), P("dp", "head"), P(), P("dp"),
    )
    return jax.shard_map(
        local, mesh=mesh, in_specs=in_specs,
        out_specs=(P("dp", "head"), P("dp", "head")), check_vma=False)
```

profile of v0, /device:TPU:0, one launch (start us, length us, event | category | flops | bytes accessed | tf_op | source)
XLA Modules:
  0.0 115.6 jit_solution(1368733778250696503)
XLA Ops:
  0.6 111.1 %shard_map.113 = (bf16[128,640]{1,0:T(8,128)(2,1)}, bf16[128,4096]{1,0:T(8,128)(2,1)}) custom-call(s32[10]{0:T(128)} %src_ref.1, s32[1,128]{1,0:T(1,128)} %bitcast.1, f32[128,128]{1,0:T(8,128)} %constant.4.clone.cos_hbm, f32[128,128]{1,0:T(8,128)} %constant.5.clone.sin_hbm, bf16[128,8192]{1,0:T(8,128)(2,1)} %x_hbm.1, bf16[512,512]{1,0:T(8,128)(2,1)} %old_hbm.1, ...), custom_call_target="tpu_custom_call" | custom-call | tf_op jit(solution)/shard_map/pallas_call | solution.py:341
  111.7 1.6 %copy.14 = bf16[128,640]{1,0:T(8,128)(2,1)} copy(bf16[128,640]{1,0:T(8,128)(2,1)} %get-tuple-element.4) | data formatting | bytes 327680
  113.3 2.3 %copy.15 = bf16[128,4096]{1,0:T(8,128)(2,1)} copy(bf16[128,4096]{1,0:T(8,128)(2,1)} %get-tuple-element.5) | data formatting | bytes 2097152
where the time goes:
time: 116 us
  Pallas kernels  111 us (96%)
  local copies, waits for them, and re-layouts  3.88 us (3%)
    pallas_call x1, Pallas kernels, local(): pl.pallas_call(functools.partial(kernel, n_dp, n_head, group, ways), out_...  111 us
    unnamed x2, local copies, waits for them, and re-layouts  3.88 us

commit v1 on v0

--- a/solution.py
+++ b/solution.py
@@ -322,6 +322,440 @@
         lax.fori_loop(0, chunks, drain_share, 0)
 
 
+def pair_kernel(
+    n_dp, group, capacity,
+    src_ref, doc_hbm, cos_hbm, sin_hbm, x_hbm, old_hbm, fresh_hbm, k_hbm, v_hbm, g_hbm,
+    out_ref, grad_ref,
+    doc_ref, cos_ref, sin_ref, x_ref, own_ref, g_ref, wq, wkv, oq, okv, parcel, arrived, accq, acckv,
+    dq_ref, dkv_ref, eq_ref, ekv_ref, psend, precv,
+    in_sem, rs, rr, cs, cr, hs, hr, ys, yr, ts, tr, ds, dr, ps, pr,
+):
+    me, head = lax.axis_index("dp"), lax.axis_index("head")
+    rows, hd = k_hbm.shape
+    length = x_ref.shape[0]
+    lanes, ways, subs = 2, 2, 2
+    m = n_dp // lanes
+    half = n_dp // 2
+    core, chip = me % lanes, me // lanes
+    side, level = chip % 2, chip // 2
+    pos = (1 - side) * level + side * (m - 1 - level)
+    piece = rows // ways
+    sub = piece // subs
+    lead = min(m // 2, m - 2)
+    near = m // 2
+    signs = (1, -1)
+    bufs = (wkv, wq)
+    others = (okv, oq)
+    parts = len(bufs) * subs
+
+    def index_of(p, lane):
+        p = (p + 2 * m) % m
+        far = p // (m // 2)
+        return ((1 - far) * 2 * p + far * (2 * (m - 1 - p) + 1)) * lanes + lane
+
+    right, left = index_of(pos + 1, core), index_of(pos - 1, core)
+    targets = (right, left)
+    partner = index_of(pos, 1 - core)
+    across_y = (me, 1 - head)
+
+    loads = [
+        pltpu.make_async_copy(k_hbm, wkv.at[me, :, pl.ds(0, hd)], in_sem.at[0]),
+        pltpu.make_async_copy(v_hbm, wkv.at[me, :, pl.ds(hd, hd)], in_sem.at[1]),
+    ]
+    loads += [
+        pltpu.make_async_copy(old_hbm.at[:, pl.ds(c * hd, hd)], own_ref.at[c], in_sem.at[2 + c])
+        for c in range(group - 1)
+    ]
+    loads += [
+        pltpu.make_async_copy(fresh_hbm, own_ref.at[group - 1], in_sem.at[group + 1]),
+        pltpu.make_async_copy(x_hbm, x_ref, in_sem.at[group + 2]),
+        pltpu.make_async_copy(g_hbm, g_ref, in_sem.at[group + 3]),
+        pltpu.make_async_copy(doc_hbm, doc_ref, in_sem.at[group + 4]),
+        pltpu.make_async_copy(cos_hbm, cos_ref, in_sem.at[group + 5]),
+        pltpu.make_async_copy(sin_hbm, sin_ref, in_sem.at[group + 6]),
+    ]
+    for load in loads:
+        load.start()
+
+    barrier = pltpu.get_barrier_semaphore()
+    peers = [(right, head), (left, head), (partner, head), across_y]
+    for peer in peers:
+        pl.semaphore_signal(barrier, inc=1, device_id=peer, device_id_type=MESH)
+
+    def remote(src, dst, send, recv, device):
+        return pltpu.make_async_remote_copy(
+            src, dst, send, recv, device_id=device, device_id_type=MESH)
+
+    def part_of(p, w, owner):
+        return bufs[p // subs].at[owner, pl.ds(w * piece + p % subs * sub, sub)]
+
+    def ring(p, w, s):
+        ref = part_of(p, w, index_of(pos - signs[w] * s, core))
+        return remote(ref, ref, rs.at[w * parts + p, s], rr.at[w * parts + p, s], (targets[w], head))
+
+    def ring_in(p, w, s):
+        ref = part_of(p, w, index_of(pos - signs[w] * (s + 1), core))
+        return remote(ref, ref, rs.at[w * parts + p, s], rr.at[w * parts + p, s], (targets[w], head))
+
+    def across(p, w, s, lane):
+        ref = part_of(p, w, index_of(pos - signs[w] * s, lane))
+        return remote(ref, ref, cs.at[w * parts + p, s], cr.at[w * parts + p, s], (partner, head))
+
+    def forward(p, w, s, to):
+        owner = index_of(pos - signs[w] * s, core)
+        dst = others[p // subs].at[owner - to * half, pl.ds(w * piece + p % subs * sub, sub)]
+        return remote(part_of(p, w, owner), dst, ys.at[w * parts + p, s], yr.at[w * parts + p, s], across_y)
+
+    def share(b, w, s, lane):
+        owner = index_of(pos - signs[w] * s, lane)
+        ref = others[b].at[owner - head * half, pl.ds(w * piece, piece)]
+        return remote(ref, ref, ts.at[w * 2 + b, s], tr.at[w * 2 + b, s], (partner, head))
+
+    def for_here(w, s):
+        return index_of(pos - signs[w] * s, core) // half == head
+
+    def relay(u):
+        return remote(parcel.at[u], arrived.at[u], hs.at[u], hr.at[u], across_y)
+
+    def hand_on(p, w, s):
+        @pl.when((s <= near) & jnp.logical_not(for_here(w, s)))
+        def _():
+            forward(p, w, s, 1 - head).start()
+
+    shift = [(2 - src_ref[k] // group) % 2 for k in range(group)]
+    taken = [src_ref[k] % group for k in range(group)]
+    slot = [
+        sum([(shift[l] == 1).astype(jnp.int32) for l in range(k)], jnp.int32(0)) * shift[k]
+        for k in range(group)
+    ]
+    units = range(ways * subs)
+
+    for load in loads[:2]:
+        load.wait()
+    pl.semaphore_wait(barrier, len(peers))
+    for p in range(subs):
+        for w in range(ways):
+            ring(p, w, 0).start()
+    for p in range(subs):
+        for w in range(ways):
+            across(p, w, 0, core).start()
+    for load in loads[2:2 + group]:
+        load.wait()
+    for c in range(capacity):
+        pick = sum([jnp.where((shift[k] == 1) & (slot[k] == c), taken[k], 0) for k in range(group)], jnp.int32(0))
+        for u in units:
+            parcel[u, c] = own_ref[pick, u * sub:(u + 1) * sub]
+    for u in units:
+        relay(u).start()
+    for p in range(subs):
+        for w in range(ways):
+            hand_on(p, w, 0)
+    for load in loads[2 + group:]:
+        load.wait()
+
+    def add(b, places):
+        acc = (acckv, accq)[b]
+        total = acc[...]
+        for w, owner in places:
+            xs = x_ref[:, pl.ds(pl.multiple_of(owner * rows + w * piece, 128), piece)]
+            total = total + dot(xs, bufs[b][owner, pl.ds(w * piece, piece), :], 1, 0)
+        acc[...] = total
+
+    def pass_on(p, w, s):
+        ring_in(p, w, s - 1).wait_recv()
+
+        @pl.when(s < m - 1)
+        def _():
+            ring(p, w, s).start()
+
+        across(p, w, s, core).start()
+        hand_on(p, w, s)
+
+    accq[...] = jnp.zeros_like(accq)
+    acckv[...] = jnp.zeros_like(acckv)
+    add(0, [(w, me) for w in range(ways)])
+    for s in range(1, lead + 1):
+        for p in range(subs):
+            for w in range(ways):
+                pass_on(p, w, s)
+        if s == lead - 1:
+            for u in units:
+                relay(u).wait_recv()
+            for u in units:
+                block = slice(u * sub, (u + 1) * sub)
+                for k in range(group):
+                    wq[me, block, k * hd:(k + 1) * hd] = jnp.where(
+                        shift[k] == 0, own_ref[taken[k], block], arrived[u, slot[k]])
+            for p in range(subs, parts):
+                for w in range(ways):
+                    ring(p, w, 0).start()
+            for p in range(subs, parts):
+                for w in range(ways):
+                    across(p, w, 0, core).start()
+                    hand_on(p, w, 0)
+    add(1, [(w, me) for w in range(ways)])
+
+    def step(s, carry):
+        @pl.when(s + lead < m)
+        def _():
+            for p in range(subs):
+                for w in range(ways):
+                    pass_on(p, w, s + lead)
+
+        for p in range(subs, parts):
+            for w in range(ways):
+                pass_on(p, w, s)
+        for w in range(ways):
+            for p in range(parts):
+                across(p, w, s - 1, 1 - core).wait_recv()
+        places = [(w, index_of(pos - signs[w] * s, core)) for w in range(ways)]
+        places += [(w, index_of(pos - signs[w] * (s - 1), 1 - core)) for w in range(ways)]
+        for b in range(2):
+            add(b, places)
+        return carry
+
+    lax.fori_loop(1, m, step, 0)
+    for w in range(ways):
+        for p in range(parts):
+            across(p, w, m - 1, 1 - core).wait_recv()
+    for b in range(2):
+        add(b, [(w, index_of(pos - signs[w] * (m - 1), 1 - core)) for w in range(ways)])
+
+    scale = 1.0 / math.sqrt(hd)
+    cosine, sine = cos_ref[...], sin_ref[...]
+
+    def rotate(f):
+        return f * cosine + pltpu.roll(f, hd // 2, 1) * sine
+
+    def rotate_back(f):
+        return f * cosine - pltpu.roll(f, hd // 2, 1) * sine
+
+    def swap_q(k):
+        cols = pl.ds(k * hd, hd)
+        return remote(dq_ref.at[:, cols], eq_ref.at[:, cols], ds.at[k], dr.at[k], across_y)
+
+    swap_kv = remote(dkv_ref, ekv_ref, ds.at[group], dr.at[group], across_y)
+
+    docs = jnp.broadcast_to(doc_ref[...].astype(jnp.float32), (length, length))
+    at_key = lax.broadcasted_iota(jnp.int32, (length, length), 1)
+    at_query = lax.broadcasted_iota(jnp.int32, (length, length), 0)
+    allowed = (at_key <= at_query) & (docs == docs.T)
+    key = rotate(acckv[:, :hd]).astype(jnp.bfloat16)
+    value = acckv[:, hd:].astype(jnp.bfloat16)
+    dkey = jnp.zeros((length, hd), jnp.float32)
+    dvalue = jnp.zeros((length, hd), jnp.float32)
+    for k in range(group):
+        cols = slice(k * hd, (k + 1) * hd)
+        query = rotate(accq[:, cols]).astype(jnp.bfloat16)
+        given = g_ref[:, cols]
+        scores = jnp.where(allowed, dot(query, key, 1, 1) * scale, neg_large)
+        weights = jnp.exp(scores - jnp.max(scores, axis=-1, keepdims=True))
+        probs = weights / jnp.sum(weights, axis=-1, keepdims=True)
+        probs_b = probs.astype(jnp.bfloat16)
+        out_ref[:, cols] = dot(probs_b, value, 1, 0).astype(jnp.bfloat16)
+        prob_grad = dot(given, value, 1, 1)
+        centre = jnp.sum(probs * prob_grad, axis=-1, keepdims=True)
+        dscore = (probs * (prob_grad - centre) * scale).astype(jnp.bfloat16)
+        dq_ref[:, cols] = rotate_back(dot(dscore, key, 1, 0)).astype(jnp.bfloat16)
+        swap_q(k).start()
+        dkey = dkey + dot(dscore, query, 0, 0)
+        dvalue = dvalue + dot(probs_b, given, 0, 0)
+    dkv_ref[:, :hd] = rotate_back(dkey).astype(jnp.bfloat16)
+    dkv_ref[:, hd:] = dvalue.astype(jnp.bfloat16)
+    swap_kv.start()
+
+    def partial(owner, w):
+        block = pl.ds(w * piece, piece)
+        return (dot(dq_ref[...], wq[owner, block, :], 1, 1)
+                + dot(dkv_ref[...], wkv[owner, block, :], 1, 1)).astype(jnp.bfloat16)
+
+    def partial_other(place, w):
+        block = pl.ds(w * piece, piece)
+        return (dot(eq_ref[...], oq[place, block, :], 1, 1)
+                + dot(ekv_ref[...], okv[place, block, :], 1, 1)).astype(jnp.bfloat16)
+
+    def send_share(w, s, lane):
+        at = (w, s - near - 1, lane)
+        return remote(psend.at[at], precv.at[at], ps.at[at], pr.at[at], across_y)
+
+    def far_steps(body):
+        def loop(s, carry):
+            for w in range(ways):
+                body(w, s)
+            return carry
+
+        lax.fori_loop(near + 1, m, loop, 0)
+
+    def near_steps(body):
+        def loop(s, carry):
+            for w in range(ways):
+                body(w, s)
+            return carry
+
+        lax.fori_loop(0, near + 1, loop, 0)
+
+    def send_far(w, s):
+        @pl.when(jnp.logical_not(for_here(w, s)))
+        def _():
+            for lane in range(lanes):
+                psend[w, s - near - 1, lane] = partial(index_of(pos - signs[w] * s, lane), w)
+                send_share(w, s, lane).start()
+
+    far_steps(send_far)
+
+    def share_near(w, s):
+        @pl.when(for_here(w, s))
+        def _():
+            for p in range(parts):
+                forward(p, w, s, head).wait_recv()
+            for b in range(2):
+                share(b, w, s, core).start()
+
+    near_steps(share_near)
+
+    def columns(owner, w):
+        return pl.ds(pl.multiple_of((owner - head * half) * rows + w * piece, 128), piece)
+
+    def own_part(i, carry):
+        owner = head * half + i
+        for w in range(ways):
+            grad_ref[:, columns(owner, w)] = partial(owner, w)
+        return carry
+
+    lax.fori_loop(0, half, own_part, 0)
+
+    for k in range(group):
+        swap_q(k).wait_recv()
+    swap_kv.wait_recv()
+
+    def plus(owner, w, value):
+        cols = columns(owner, w)
+        grad_ref[:, cols] = (grad_ref[:, cols].astype(jnp.float32) + value.astype(jnp.float32)).astype(jnp.bfloat16)
+
+    def add_near(w, s):
+        @pl.when(for_here(w, s))
+        def _():
+            for b in range(2):
+                share(b, w, s, 1 - core).wait_recv()
+            for lane in range(lanes):
+                owner = index_of(pos - signs[w] * s, lane)
+                plus(owner, w, partial_other(owner - head * half, w))
+
+    near_steps(add_near)
+
+    def add_far(w, s):
+        @pl.when(for_here(w, s))
+        def _():
+            for lane in range(lanes):
+                send_share(w, s, lane).wait_recv()
+                plus(index_of(pos - signs[w] * s, lane), w, precv[w, s - near - 1, lane])
+
+    far_steps(add_far)
+
+    def drain(s, carry):
+        for w in range(ways):
+            for p in range(parts):
+                @pl.when(s < m - 1)
+                def _():
+                    ring(p, w, s).wait_send()
+
+                across(p, w, s, core).wait_send()
+        return carry
+
+    lax.fori_loop(0, m, drain, 0)
+
+    def drain_near(w, s):
+        @pl.when(jnp.logical_not(for_here(w, s)))
+        def _():
+            for p in range(parts):
+                forward(p, w, s, 1 - head).wait_send()
+
+        @pl.when(for_here(w, s))
+        def _():
+            for b in range(2):
+                share(b, w, s, core).wait_send()
+
+    near_steps(drain_near)
+
+    def drain_far(w, s):
+        @pl.when(jnp.logical_not(for_here(w, s)))
+        def _():
+            for lane in range(lanes):
+                send_share(w, s, lane).wait_send()
+
+    far_steps(drain_far)
+    for u in units:
+        relay(u).wait_send()
+    for k in range(group):
+        swap_q(k).wait_send()
+    swap_kv.wait_send()
+
+
+def pair_call(n_dp, x, old, fresh, wk, wv, g, head_source, doc_ids):
+    length, width = x.shape
+    rows, hd = wk.shape
+    group = g.shape[1] // hd
+    m, half, ways, subs = n_dp // 2, n_dp // 2, 2, 2
+    near = m // 2
+    capacity = (group + 1) // 2
+    cosine, sine = rotary_tables(length, hd)
+    bf, f32 = jnp.bfloat16, jnp.float32
+    vm = pl.BlockSpec(memory_space=pltpu.VMEM)
+    anyspace = pl.BlockSpec(memory_space=pl.ANY)
+    dma = pltpu.SemaphoreType.DMA
+    units, unit = ways * subs, rows // (ways * subs)
+    parts = 2 * subs
+    far = (ways, m - 1 - near, 2)
+    return pl.pallas_call(
+        functools.partial(pair_kernel, n_dp, group, capacity),
+        out_shape=(
+            jax.ShapeDtypeStruct((length, group * hd), bf),
+            jax.ShapeDtypeStruct((length, width // 2), bf),
+        ),
+        in_specs=[pl.BlockSpec(memory_space=pltpu.SMEM)] + [anyspace] * 9,
+        out_specs=(vm, vm),
+        scratch_shapes=[
+            pltpu.VMEM((1, length), jnp.int32),
+            pltpu.VMEM((length, hd), f32),
+            pltpu.VMEM((length, hd), f32),
+            pltpu.VMEM((length, width), bf),
+            pltpu.VMEM((group, rows, hd), bf),
+            pltpu.VMEM((length, group * hd), bf),
+            pltpu.VMEM((n_dp, rows, group * hd), bf),
+            pltpu.VMEM((n_dp, rows, 2 * hd), bf),
+            pltpu.VMEM((half, rows, group * hd), bf),
+            pltpu.VMEM((half, rows, 2 * hd), bf),
+            pltpu.VMEM((units, capacity, unit, hd), bf),
+            pltpu.VMEM((units, capacity, unit, hd), bf),
+            pltpu.VMEM((length, group * hd), f32),
+            pltpu.VMEM((length, 2 * hd), f32),
+            pltpu.VMEM((length, group * hd), bf),
+            pltpu.VMEM((length, 2 * hd), bf),
+            pltpu.VMEM((length, group * hd), bf),
+            pltpu.VMEM((length, 2 * hd), bf),
+            pltpu.VMEM(far + (length, rows // ways), bf),
+            pltpu.VMEM(far + (length, rows // ways), bf),
+            dma((group + 7,)),
+            dma((parts * ways, m)),
+            dma((parts * ways, m)),
+            dma((parts * ways, m)),
+            dma((parts * ways, m)),
+            dma((units,)),
+            dma((units,)),
+            dma((parts * ways, near + 1)),
+            dma((parts * ways, near + 1)),
+            dma((2 * ways, near + 1)),
+            dma((2 * ways, near + 1)),
+            dma((group + 1,)),
+            dma((group + 1,)),
+            dma(far),
+            dma(far),
+        ],
+        compiler_params=pltpu.CompilerParams(
+            collective_id=0, has_side_effects=True, vmem_limit_bytes=67043328),
+    )(head_source, doc_ids.reshape(1, -1), cosine, sine, x, old, fresh, wk, wv, g)
+
+
 def solution(mesh):
     n_dp, n_head = mesh.shape["dp"], mesh.shape["head"]
 
@@ -331,6 +765,8 @@
         group = g.shape[1] // hd
         ways = 2 if rows % 256 == 0 else 1
         m = n_dp // 2
+        if n_head == 2 and rows % 512 == 0 and m % 4 == 0:
+            return pair_call(n_dp, x, old, fresh, wk, wv, g, head_source, doc_ids)
         capacity = (group + n_head - 1) // n_head
         chunks = n_dp // n_head
         cosine, sine = rotary_tables(length, hd)

time: 116 us -> 106 us (0.914)
  Pallas kernels: 111 us -> 101 us
    pallas_call x1, Pallas kernels: 111 us -> 101 us  [pair_call(): pl.pallas_call(functools.partial(pair_kernel, n_dp, group, capacity), out...]
where the time goes in v1:
time: 106 us
  Pallas kernels  101 us (95%)
  local copies, waits for them, and re-layouts  3.88 us (4%)
    pallas_call x1, Pallas kernels, pair_call(): pl.pallas_call(functools.partial(pair_kernel, n_dp, group, capacity), out...  101 us
    unnamed x2, local copies, waits for them, and re-layouts  3.88 us

profile of v1, /device:TPU:0, one launch (start us, length us, event | category | flops | bytes accessed | tf_op | source)
XLA Modules:
  0.0 105.8 jit_solution(12890144560455218953)
XLA Ops:
  0.6 101.3 %shard_map.113 = (bf16[128,640]{1,0:T(8,128)(2,1)}, bf16[128,4096]{1,0:T(8,128)(2,1)}) custom-call(s32[10]{0:T(128)} %src_ref.1, s32[1,128]{1,0:T(1,128)} %bitcast.1, f32[128,128]{1,0:T(8,128)} %constant.4.clone.cos_hbm, f32[128,128]{1,0:T(8,128)} %constant.5.clone.sin_hbm, bf16[128,8192]{1,0:T(8,128)(2,1)} %x_hbm.1, bf16[512,512]{1,0:T(8,128)(2,1)} %old_hbm.1, ...), custom_call_target="tpu_custom_call" | custom-call | tf_op jit(solution)/shard_map/pallas_call | solution.py:709
  101.9 1.6 %copy.14 = bf16[128,640]{1,0:T(8,128)(2,1)} copy(bf16[128,640]{1,0:T(8,128)(2,1)} %get-tuple-element.4) | data formatting | bytes 327680
  103.5 2.3 %copy.15 = bf16[128,4096]{1,0:T(8,128)(2,1)} copy(bf16[128,4096]{1,0:T(8,128)(2,1)} %get-tuple-element.5) | data formatting | bytes 2097152

commit v2 on v1

--- a/solution.py
+++ b/solution.py
@@ -391,31 +391,39 @@
 
     def ring(p, w, s):
         ref = part_of(p, w, index_of(pos - signs[w] * s, core))
-        return remote(ref, ref, rs.at[w * parts + p, s], rr.at[w * parts + p, s], (targets[w], head))
-
-    def ring_in(p, w, s):
-        ref = part_of(p, w, index_of(pos - signs[w] * (s + 1), core))
-        return remote(ref, ref, rs.at[w * parts + p, s], rr.at[w * parts + p, s], (targets[w], head))
+        return remote(ref, ref, rs.at[p // subs], rr.at[p, s], (targets[w], head))
+
+    def ring_in(p, s):
+        ref = bufs[p // subs].at[me, pl.ds(0, ways * sub)]
+        return remote(ref, ref, rs.at[p // subs], rr.at[p, s], (left, head))
 
     def across(p, w, s, lane):
         ref = part_of(p, w, index_of(pos - signs[w] * s, lane))
-        return remote(ref, ref, cs.at[w * parts + p, s], cr.at[w * parts + p, s], (partner, head))
+        return remote(ref, ref, cs.at[p // subs], cr.at[p // subs, s], (partner, head))
+
+    def across_in(b, s):
+        ref = bufs[b].at[me]
+        return remote(ref, ref, cs.at[b], cr.at[b, s], (partner, head))
 
     def forward(p, w, s, to):
         owner = index_of(pos - signs[w] * s, core)
         dst = others[p // subs].at[owner - to * half, pl.ds(w * piece + p % subs * sub, sub)]
-        return remote(part_of(p, w, owner), dst, ys.at[w * parts + p, s], yr.at[w * parts + p, s], across_y)
+        return remote(part_of(p, w, owner), dst, ys.at[p // subs], yr.at[p // subs], across_y)
 
     def share(b, w, s, lane):
         owner = index_of(pos - signs[w] * s, lane)
         ref = others[b].at[owner - head * half, pl.ds(w * piece, piece)]
-        return remote(ref, ref, ts.at[w * 2 + b, s], tr.at[w * 2 + b, s], (partner, head))
+        return remote(ref, ref, ts.at[b], tr.at[b], (partner, head))
+
+    def all_of(b, count, send, recv):
+        ref = bufs[b].at[pl.ds(0, count), pl.ds(0, piece)]
+        return remote(ref, ref, send.at[b], recv.at[b], across_y)
 
     def for_here(w, s):
         return index_of(pos - signs[w] * s, core) // half == head
 
     def relay(u):
-        return remote(parcel.at[u], arrived.at[u], hs.at[u], hr.at[u], across_y)
+        return remote(parcel.at[u], arrived.at[u], hs.at[0], hr.at[0], across_y)
 
     def hand_on(p, w, s):
         @pl.when((s <= near) & jnp.logical_not(for_here(w, s)))
@@ -461,26 +469,26 @@
             total = total + dot(xs, bufs[b][owner, pl.ds(w * piece, piece), :], 1, 0)
         acc[...] = total
 
-    def pass_on(p, w, s):
-        ring_in(p, w, s - 1).wait_recv()
+    def pass_on(p, s):
+        ring_in(p, s - 1).wait_recv()
 
         @pl.when(s < m - 1)
         def _():
-            ring(p, w, s).start()
-
-        across(p, w, s, core).start()
-        hand_on(p, w, s)
+            for w in range(ways):
+                ring(p, w, s).start()
+
+        for w in range(ways):
+            across(p, w, s, core).start()
+            hand_on(p, w, s)
 
     accq[...] = jnp.zeros_like(accq)
     acckv[...] = jnp.zeros_like(acckv)
     add(0, [(w, me) for w in range(ways)])
     for s in range(1, lead + 1):
         for p in range(subs):
-            for w in range(ways):
-                pass_on(p, w, s)
+            pass_on(p, s)
         if s == lead - 1:
-            for u in units:
-                relay(u).wait_recv()
+            remote(parcel, arrived, hs.at[0], hr.at[0], across_y).wait_recv()
             for u in units:
                 block = slice(u * sub, (u + 1) * sub)
                 for k in range(group):
@@ -499,15 +507,12 @@
         @pl.when(s + lead < m)
         def _():
             for p in range(subs):
-                for w in range(ways):
-                    pass_on(p, w, s + lead)
+                pass_on(p, s + lead)
 
         for p in range(subs, parts):
-            for w in range(ways):
-                pass_on(p, w, s)
-        for w in range(ways):
-            for p in range(parts):
-                across(p, w, s - 1, 1 - core).wait_recv()
+            pass_on(p, s)
+        for b in range(2):
+            across_in(b, s - 1).wait_recv()
         places = [(w, index_of(pos - signs[w] * s, core)) for w in range(ways)]
         places += [(w, index_of(pos - signs[w] * (s - 1), 1 - core)) for w in range(ways)]
         for b in range(2):
@@ -515,10 +520,8 @@
         return carry
 
     lax.fori_loop(1, m, step, 0)
-    for w in range(ways):
-        for p in range(parts):
-            across(p, w, m - 1, 1 - core).wait_recv()
     for b in range(2):
+        across_in(b, m - 1).wait_recv()
         add(b, [(w, index_of(pos - signs[w] * (m - 1), 1 - core)) for w in range(ways)])
 
     scale = 1.0 / math.sqrt(hd)
@@ -532,9 +535,10 @@
 
     def swap_q(k):
         cols = pl.ds(k * hd, hd)
-        return remote(dq_ref.at[:, cols], eq_ref.at[:, cols], ds.at[k], dr.at[k], across_y)
-
-    swap_kv = remote(dkv_ref, ekv_ref, ds.at[group], dr.at[group], across_y)
+        return remote(dq_ref.at[:, cols], eq_ref.at[:, cols], ds.at[0], dr.at[0], across_y)
+
+    swap_kv = remote(dkv_ref, ekv_ref, ds.at[1], dr.at[1], across_y)
+    swap_all_q = remote(dq_ref, eq_ref, ds.at[0], dr.at[0], across_y)
 
     docs = jnp.broadcast_to(doc_ref[...].astype(jnp.float32), (length, length))
     at_key = lax.broadcasted_iota(jnp.int32, (length, length), 1)
@@ -576,7 +580,7 @@
 
     def send_share(w, s, lane):
         at = (w, s - near - 1, lane)
-        return remote(psend.at[at], precv.at[at], ps.at[at], pr.at[at], across_y)
+        return remote(psend.at[at], precv.at[at], ps.at[0], pr.at[at], across_y)
 
     def far_steps(body):
         def loop(s, carry):
@@ -603,11 +607,12 @@
 
     far_steps(send_far)
 
+    for b in range(2):
+        all_of(b, near + 1, ys, yr).wait_recv()
+
     def share_near(w, s):
         @pl.when(for_here(w, s))
         def _():
-            for p in range(parts):
-                forward(p, w, s, head).wait_recv()
             for b in range(2):
                 share(b, w, s, core).start()
 
@@ -624,9 +629,10 @@
 
     lax.fori_loop(0, half, own_part, 0)
 
-    for k in range(group):
-        swap_q(k).wait_recv()
+    swap_all_q.wait_recv()
     swap_kv.wait_recv()
+    for b in range(2):
+        all_of(b, near + 1, ts, tr).wait_recv()
 
     def plus(owner, w, value):
         cols = columns(owner, w)
@@ -635,8 +641,6 @@
     def add_near(w, s):
         @pl.when(for_here(w, s))
         def _():
-            for b in range(2):
-                share(b, w, s, 1 - core).wait_recv()
             for lane in range(lanes):
                 owner = index_of(pos - signs[w] * s, lane)
                 plus(owner, w, partial_other(owner - head * half, w))
@@ -652,43 +656,14 @@
 
     far_steps(add_far)
 
-    def drain(s, carry):
-        for w in range(ways):
-            for p in range(parts):
-                @pl.when(s < m - 1)
-                def _():
-                    ring(p, w, s).wait_send()
-
-                across(p, w, s, core).wait_send()
-        return carry
-
-    lax.fori_loop(0, m, drain, 0)
-
-    def drain_near(w, s):
-        @pl.when(jnp.logical_not(for_here(w, s)))
-        def _():
-            for p in range(parts):
-                forward(p, w, s, 1 - head).wait_send()
-
-        @pl.when(for_here(w, s))
-        def _():
-            for b in range(2):
-                share(b, w, s, core).wait_send()
-
-    near_steps(drain_near)
-
-    def drain_far(w, s):
-        @pl.when(jnp.logical_not(for_here(w, s)))
-        def _():
-            for lane in range(lanes):
-                send_share(w, s, lane).wait_send()
-
-    far_steps(drain_far)
-    for u in units:
-        relay(u).wait_send()
-    for k in range(group):
-        swap_q(k).wait_send()
+    for b in range(2):
+        for count, sent in ((ways * (m - 1), rs), (ways * m, cs), (near + 1, ys), (near + 1, ts)):
+            all_of(b, count, sent, sent).wait_send()
+    remote(parcel, arrived, hs.at[0], hr.at[0], across_y).wait_send()
+    swap_all_q.wait_send()
     swap_kv.wait_send()
+    ref = psend.at[:, :, 0]
+    remote(ref, ref, ps.at[0], ps.at[0], across_y).wait_send()
 
 
 def pair_call(n_dp, x, old, fresh, wk, wv, g, head_source, doc_ids):
@@ -736,19 +711,19 @@
             pltpu.VMEM(far + (length, rows // ways), bf),
             pltpu.VMEM(far + (length, rows // ways), bf),
             dma((group + 7,)),
-            dma((parts * ways, m)),
-            dma((parts * ways, m)),
-            dma((parts * ways, m)),
-            dma((parts * ways, m)),
-            dma((units,)),
-            dma((units,)),
-            dma((parts * ways, near + 1)),
-            dma((parts * ways, near + 1)),
-            dma((2 * ways, near + 1)),
-            dma((2 * ways, near + 1)),
-            dma((group + 1,)),
-            dma((group + 1,)),
-            dma(far),
+            dma((2,)),
+            dma((parts, m)),
+            dma((2,)),
+            dma((2, m)),
+            dma((1,)),
+            dma((1,)),
+            dma((2,)),
+            dma((2,)),
+            dma((2,)),
+            dma((2,)),
+            dma((2,)),
+            dma((2,)),
+            dma((1,)),
             dma(far),
         ],
         compiler_params=pltpu.CompilerParams(

time: 106 us -> 101 us (0.953)
  Pallas kernels: 101 us -> 96.8 us
    pallas_call x1, Pallas kernels: 101 us -> 96.8 us  [pair_call(): pl.pallas_call(functools.partial(pair_kernel, n_dp, group, capacity), out...]
where the time goes in v2:
time: 101 us
  Pallas kernels  96.8 us (96%)
  local copies, waits for them, and re-layouts  3.88 us (4%)
    pallas_call x1, Pallas kernels, pair_call(): pl.pallas_call(functools.partial(pair_kernel, n_dp, group, capacity), out...  96.8 us
    unnamed x2, local copies, waits for them, and re-layouts  3.88 us

profile of v2, /device:TPU:0, one launch (start us, length us, event | category | flops | bytes accessed | tf_op | source)
XLA Modules:
  0.0 101.3 jit_solution(1409914071039599186)
XLA Ops:
  0.6 96.8 %shard_map.113 = (bf16[128,640]{1,0:T(8,128)(2,1)}, bf16[128,4096]{1,0:T(8,128)(2,1)}) custom-call(s32[10]{0:T(128)} %src_ref.1, s32[1,128]{1,0:T(1,128)} %bitcast.1, f32[128,128]{1,0:T(8,128)} %constant.4.clone.cos_hbm, f32[128,128]{1,0:T(8,128)} %constant.5.clone.sin_hbm, bf16[128,8192]{1,0:T(8,128)(2,1)} %x_hbm.1, bf16[512,512]{1,0:T(8,128)(2,1)} %old_hbm.1, ...), custom_call_target="tpu_custom_call" | custom-call | tf_op jit(solution)/shard_map/pallas_call | solution.py:684
  97.4 1.6 %copy.14 = bf16[128,640]{1,0:T(8,128)(2,1)} copy(bf16[128,640]{1,0:T(8,128)(2,1)} %get-tuple-element.4) | data formatting | bytes 327680
  99.0 2.3 %copy.15 = bf16[128,4096]{1,0:T(8,128)(2,1)} copy(bf16[128,4096]{1,0:T(8,128)(2,1)} %get-tuple-element.5) | data formatting | bytes 2097152

commit v3 on v2

--- a/solution.py
+++ b/solution.py
@@ -684,8 +684,8 @@
     return pl.pallas_call(
         functools.partial(pair_kernel, n_dp, group, capacity),
         out_shape=(
-            jax.ShapeDtypeStruct((length, group * hd), bf),
-            jax.ShapeDtypeStruct((length, width // 2), bf),
+            pltpu.VMEM((length, group * hd), bf),
+            pltpu.VMEM((length, width // 2), bf),
         ),
         in_specs=[pl.BlockSpec(memory_space=pltpu.SMEM)] + [anyspace] * 9,
         out_specs=(vm, vm),
@@ -727,8 +727,9 @@
             dma(far),
         ],
         compiler_params=pltpu.CompilerParams(
-            collective_id=0, has_side_effects=True, vmem_limit_bytes=67043328),
-    )(head_source, doc_ids.reshape(1, -1), cosine, sine, x, old, fresh, wk, wv, g)
+            collective_id=0, has_side_effects=True, vmem_limit_bytes=48*1024*1024),
+    )(*(pltpu.with_memory_space_constraint(jnp.asarray(a), pltpu.HBM) for a in (
+        head_source, doc_ids.reshape(1, -1), cosine, sine, x, old, fresh, wk, wv, g)))
 
 
 def solution(mesh):

time: 101 us -> 98.2 us (0.972)
  local copies, waits for them, and re-layouts: 3.88 us -> 1.64 us
  Pallas kernels: 96.8 us -> 95.7 us
    unnamed x2, local copies, waits for them, and re-layouts: 3.88 us -> 1.64 us
    pallas_call x1, Pallas kernels: 96.8 us -> 95.7 us  [pair_call(): pl.pallas_call(functools.partial(pair_kernel, n_dp, group, capacity), out...]
where the time goes in v3:
time: 98.2 us; the launch traced here: 98 us
  Pallas kernels  95.7 us (97%)
  local copies, waits for them, and re-layouts  1.64 us (2%)
    pallas_call x1, Pallas kernels, pair_call(): pl.pallas_call(functools.partial(pair_kernel, n_dp, group, capacity), out...  95.7 us

profile of v3, /device:TPU:0, one launch (start us, length us, event | category | flops | bytes accessed | tf_op | source)
XLA Modules:
  0.0 98.0 jit_solution(1097618695649353278)
XLA Ops:
  0.6 95.7 %shard_map.113 = (bf16[128,640]{1,0:T(8,128)(2,1)S(1)}, bf16[128,4096]{1,0:T(8,128)(2,1)S(1)}) custom-call(s32[10]{0:T(128)} %src_ref.1, s32[1,128]{1,0:T(1,128)} %bitcast.1, f32[128,128]{1,0:T(8,128)} %constant.4.clone.cos_hbm, f32[128,128]{1,0:T(8,128)} %constant.5.clone.sin_hbm, bf16[128,8192]{1,0:T(8,128)(2,1)} %x_hbm.1, bf16[512,512]{1,0:T(8,128)(2,1)} %old_hbm.1, ...), custom_call_target="tpu_custom_call" | custom-call | tf_op jit(solution)/shard_map/pallas_call | solution.py:684
  96.4 0.7 copy.14
  97.0 1.0 copy.15

commit v4 on v3

--- a/solution.py
+++ b/solution.py
@@ -333,20 +333,24 @@
     me, head = lax.axis_index("dp"), lax.axis_index("head")
     rows, hd = k_hbm.shape
     length = x_ref.shape[0]
-    lanes, ways, subs = 2, 2, 2
+    lanes, ways = 2, 2
     m = n_dp // lanes
     half = n_dp // 2
     core, chip = me % lanes, me // lanes
     side, level = chip % 2, chip // 2
     pos = (1 - side) * level + side * (m - 1 - level)
     piece = rows // ways
-    sub = piece // subs
+    kv_parts = [(0, first, piece // 4) for first in range(0, piece, piece // 4)]
+    q_parts = [(1, first, piece // 2) for first in range(0, piece, piece // 2)]
+    parts = kv_parts + q_parts
+    kv_range, q_range = range(len(kv_parts)), range(len(kv_parts), len(parts))
+    unit = rows // parcel.shape[0]
     lead = min(m // 2, m - 2)
-    near = m // 2
+    far = m // 2 + 1
+    count = m - m // 4
     signs = (1, -1)
     bufs = (wkv, wq)
     others = (okv, oq)
-    parts = len(bufs) * subs
 
     def index_of(p, lane):
         p = (p + 2 * m) % m
@@ -387,19 +391,21 @@
             src, dst, send, recv, device_id=device, device_id_type=MESH)
 
     def part_of(p, w, owner):
-        return bufs[p // subs].at[owner, pl.ds(w * piece + p % subs * sub, sub)]
+        b, first, size = parts[p]
+        return bufs[b].at[owner, pl.ds(w * piece + first, size)]
 
     def ring(p, w, s):
         ref = part_of(p, w, index_of(pos - signs[w] * s, core))
-        return remote(ref, ref, rs.at[p // subs], rr.at[p, s], (targets[w], head))
+        return remote(ref, ref, rs.at[parts[p][0]], rr.at[p, s], (targets[w], head))
 
     def ring_in(p, s):
-        ref = bufs[p // subs].at[me, pl.ds(0, ways * sub)]
-        return remote(ref, ref, rs.at[p // subs], rr.at[p, s], (left, head))
+        b, _, size = parts[p]
+        ref = bufs[b].at[me, pl.ds(0, ways * size)]
+        return remote(ref, ref, rs.at[b], rr.at[p, s], (left, head))
 
     def across(p, w, s, lane):
         ref = part_of(p, w, index_of(pos - signs[w] * s, lane))
-        return remote(ref, ref, cs.at[p // subs], cr.at[p // subs, s], (partner, head))
+        return remote(ref, ref, cs.at[parts[p][0]], cr.at[parts[p][0], s], (partner, head))
 
     def across_in(b, s):
         ref = bufs[b].at[me]
@@ -407,8 +413,9 @@
 
     def forward(p, w, s, to):
         owner = index_of(pos - signs[w] * s, core)
-        dst = others[p // subs].at[owner - to * half, pl.ds(w * piece + p % subs * sub, sub)]
-        return remote(part_of(p, w, owner), dst, ys.at[p // subs], yr.at[p // subs], across_y)
+        b, first, size = parts[p]
+        dst = others[b].at[owner - to * half, pl.ds(w * piece + first, size)]
+        return remote(part_of(p, w, owner), dst, ys.at[b], yr.at[b], across_y)
 
     def share(b, w, s, lane):
         owner = index_of(pos - signs[w] * s, lane)
@@ -422,11 +429,37 @@
     def for_here(w, s):
         return index_of(pos - signs[w] * s, core) // half == head
 
+    def last_forwarded(to):
+        begin = (2 * to + 3) * (m // 4)
+        steps = [[(signs[w] * (pos - begin - i) + 3 * m) % m for i in range(m // 2)] for w in range(ways)]
+        limits = []
+        for w in range(ways):
+            limit = jnp.int32(-1)
+            for s in steps[w]:
+                later = sum([(t > s - (v > w)).astype(jnp.int32) for v in range(ways) for t in steps[v]], jnp.int32(0))
+                limit = jnp.maximum(limit, jnp.where(later >= m // 4, s, -1))
+            limits.append(limit)
+        return limits
+
+    limit_out, limit_in = last_forwarded(1 - head), last_forwarded(head)
+
+    def forwarded(w, s):
+        return jnp.logical_not(for_here(w, s)) & (s <= limit_out[w])
+
+    def received(w, s):
+        return for_here(w, s) & (s <= limit_in[w])
+
+    def shared_out(w, s):
+        return jnp.logical_not(for_here(w, s)) & (s > limit_out[w])
+
+    def shared_in(w, s):
+        return for_here(w, s) & (s > limit_in[w])
+
     def relay(u):
         return remote(parcel.at[u], arrived.at[u], hs.at[0], hr.at[0], across_y)
 
     def hand_on(p, w, s):
-        @pl.when((s <= near) & jnp.logical_not(for_here(w, s)))
+        @pl.when(forwarded(w, s))
         def _():
             forward(p, w, s, 1 - head).start()
 
@@ -436,15 +469,15 @@
         sum([(shift[l] == 1).astype(jnp.int32) for l in range(k)], jnp.int32(0)) * shift[k]
         for k in range(group)
     ]
-    units = range(ways * subs)
+    units = range(parcel.shape[0])
 
     for load in loads[:2]:
         load.wait()
     pl.semaphore_wait(barrier, len(peers))
-    for p in range(subs):
+    for p in kv_range:
         for w in range(ways):
             ring(p, w, 0).start()
-    for p in range(subs):
+    for p in kv_range:
         for w in range(ways):
             across(p, w, 0, core).start()
     for load in loads[2:2 + group]:
@@ -452,10 +485,10 @@
     for c in range(capacity):
         pick = sum([jnp.where((shift[k] == 1) & (slot[k] == c), taken[k], 0) for k in range(group)], jnp.int32(0))
         for u in units:
-            parcel[u, c] = own_ref[pick, u * sub:(u + 1) * sub]
+            parcel[u, c] = own_ref[pick, u * unit:(u + 1) * unit]
     for u in units:
         relay(u).start()
-    for p in range(subs):
+    for p in kv_range:
         for w in range(ways):
             hand_on(p, w, 0)
     for load in loads[2 + group:]:
@@ -485,19 +518,19 @@
     acckv[...] = jnp.zeros_like(acckv)
     add(0, [(w, me) for w in range(ways)])
     for s in range(1, lead + 1):
-        for p in range(subs):
+        for p in kv_range:
             pass_on(p, s)
         if s == lead - 1:
             remote(parcel, arrived, hs.at[0], hr.at[0], across_y).wait_recv()
             for u in units:
-                block = slice(u * sub, (u + 1) * sub)
+                block = slice(u * unit, (u + 1) * unit)
                 for k in range(group):
                     wq[me, block, k * hd:(k + 1) * hd] = jnp.where(
                         shift[k] == 0, own_ref[taken[k], block], arrived[u, slot[k]])
-            for p in range(subs, parts):
+            for p in q_range:
                 for w in range(ways):
                     ring(p, w, 0).start()
-            for p in range(subs, parts):
+            for p in q_range:
                 for w in range(ways):
                     across(p, w, 0, core).start()
                     hand_on(p, w, 0)
@@ -506,10 +539,10 @@
     def step(s, carry):
         @pl.when(s + lead < m)
         def _():
-            for p in range(subs):
+            for p in kv_range:
                 pass_on(p, s + lead)
 
-        for p in range(subs, parts):
+        for p in q_range:
             pass_on(p, s)
         for b in range(2):
             across_in(b, s - 1).wait_recv()
@@ -579,44 +612,36 @@
                 + dot(ekv_ref[...], okv[place, block, :], 1, 1)).astype(jnp.bfloat16)
 
     def send_share(w, s, lane):
-        at = (w, s - near - 1, lane)
+        at = (w, s - far, lane)
         return remote(psend.at[at], precv.at[at], ps.at[0], pr.at[at], across_y)
 
-    def far_steps(body):
+    def each_step(body, first=0):
         def loop(s, carry):
             for w in range(ways):
                 body(w, s)
             return carry
 
-        lax.fori_loop(near + 1, m, loop, 0)
-
-    def near_steps(body):
-        def loop(s, carry):
-            for w in range(ways):
-                body(w, s)
-            return carry
-
-        lax.fori_loop(0, near + 1, loop, 0)
+        lax.fori_loop(first, m, loop, 0)
 
     def send_far(w, s):
-        @pl.when(jnp.logical_not(for_here(w, s)))
+        @pl.when(shared_out(w, s))
         def _():
             for lane in range(lanes):
-                psend[w, s - near - 1, lane] = partial(index_of(pos - signs[w] * s, lane), w)
+                psend[w, s - far, lane] = partial(index_of(pos - signs[w] * s, lane), w)
                 send_share(w, s, lane).start()
 
-    far_steps(send_far)
+    each_step(send_far, far)
 
     for b in range(2):
-        all_of(b, near + 1, ys, yr).wait_recv()
+        all_of(b, count, ys, yr).wait_recv()
 
     def share_near(w, s):
-        @pl.when(for_here(w, s))
+        @pl.when(received(w, s))
         def _():
             for b in range(2):
                 share(b, w, s, core).start()
 
-    near_steps(share_near)
+    each_step(share_near)
 
     def columns(owner, w):
         return pl.ds(pl.multiple_of((owner - head * half) * rows + w * piece, 128), piece)
@@ -632,37 +657,37 @@
     swap_all_q.wait_recv()
     swap_kv.wait_recv()
     for b in range(2):
-        all_of(b, near + 1, ts, tr).wait_recv()
+        all_of(b, count, ts, tr).wait_recv()
 
     def plus(owner, w, value):
         cols = columns(owner, w)
         grad_ref[:, cols] = (grad_ref[:, cols].astype(jnp.float32) + value.astype(jnp.float32)).astype(jnp.bfloat16)
 
     def add_near(w, s):
-        @pl.when(for_here(w, s))
+        @pl.when(received(w, s))
         def _():
             for lane in range(lanes):
                 owner = index_of(pos - signs[w] * s, lane)
                 plus(owner, w, partial_other(owner - head * half, w))
 
-    near_steps(add_near)
+    each_step(add_near)
 
     def add_far(w, s):
-        @pl.when(for_here(w, s))
+        @pl.when(shared_in(w, s))
         def _():
             for lane in range(lanes):
                 send_share(w, s, lane).wait_recv()
-                plus(index_of(pos - signs[w] * s, lane), w, precv[w, s - near - 1, lane])
-
-    far_steps(add_far)
+                plus(index_of(pos - signs[w] * s, lane), w, precv[w, s - far, lane])
+
+    each_step(add_far, far)
 
     for b in range(2):
-        for count, sent in ((ways * (m - 1), rs), (ways * m, cs), (near + 1, ys), (near + 1, ts)):
-            all_of(b, count, sent, sent).wait_send()
+        for number, sent in ((ways * (m - 1), rs), (ways * m, cs), (count, ys), (count, ts)):
+            all_of(b, number, sent, sent).wait_send()
     remote(parcel, arrived, hs.at[0], hr.at[0], across_y).wait_send()
     swap_all_q.wait_send()
     swap_kv.wait_send()
-    ref = psend.at[:, :, 0]
+    ref = psend.at[:, pl.ds(0, m // 8)]
     remote(ref, ref, ps.at[0], ps.at[0], across_y).wait_send()
 
 
@@ -670,17 +695,15 @@
     length, width = x.shape
     rows, hd = wk.shape
     group = g.shape[1] // hd
-    m, half, ways, subs = n_dp // 2, n_dp // 2, 2, 2
-    near = m // 2
+    m, half, ways, units, parts = n_dp // 2, n_dp // 2, 2, 4, 6
     capacity = (group + 1) // 2
     cosine, sine = rotary_tables(length, hd)
     bf, f32 = jnp.bfloat16, jnp.float32
     vm = pl.BlockSpec(memory_space=pltpu.VMEM)
     anyspace = pl.BlockSpec(memory_space=pl.ANY)
     dma = pltpu.SemaphoreType.DMA
-    units, unit = ways * subs, rows // (ways * subs)
-    parts = 2 * subs
-    far = (ways, m - 1 - near, 2)
+    unit = rows // units
+    far = (ways, m - 1 - m // 2, 2)
     return pl.pallas_call(
         functools.partial(pair_kernel, n_dp, group, capacity),
         out_shape=(
@@ -741,7 +764,7 @@
         group = g.shape[1] // hd
         ways = 2 if rows % 256 == 0 else 1
         m = n_dp // 2
-        if n_head == 2 and rows % 512 == 0 and m % 4 == 0:
+        if n_head == 2 and rows % 512 == 0 and m % 8 == 0:
             return pair_call(n_dp, x, old, fresh, wk, wv, g, head_source, doc_ids)
         capacity = (group + n_head - 1) // n_head
         chunks = n_dp // n_head

time: 98.2 us -> 94.9 us (0.966)
  Pallas kernels: 95.7 us -> 92.5 us
    pallas_call x1, Pallas kernels: 95.7 us -> 92.5 us  [pair_call(): pl.pallas_call(functools.partial(pair_kernel, n_dp, group, capacity), out...]
where the time goes in v4:
time: 94.9 us; the launch traced here: 94.8 us
  Pallas kernels  92.5 us (97%)
  local copies, waits for them, and re-layouts  1.64 us (2%)
    pallas_call x1, Pallas kernels, pair_call(): pl.pallas_call(functools.partial(pair_kernel, n_dp, group, capacity), out...  92.5 us

profile of v4, /device:TPU:0, one launch (start us, length us, event | category | flops | bytes accessed | tf_op | source)
XLA Modules:
  0.0 94.8 jit_solution(14579417169330795992)
XLA Ops:
  0.6 92.5 %shard_map.113 = (bf16[128,640]{1,0:T(8,128)(2,1)S(1)}, bf16[128,4096]{1,0:T(8,128)(2,1)S(1)}) custom-call(s32[10]{0:T(128)} %src_ref.1, s32[1,128]{1,0:T(1,128)} %bitcast.1, f32[128,128]{1,0:T(8,128)} %constant.4.clone.cos_hbm, f32[128,128]{1,0:T(8,128)} %constant.5.clone.sin_hbm, bf16[128,8192]{1,0:T(8,128)(2,1)} %x_hbm.1, bf16[512,512]{1,0:T(8,128)(2,1)} %old_hbm.1, ...), custom_call_target="tpu_custom_call" | custom-call | tf_op jit(solution)/shard_map/pallas_call | solution.py:707
  93.1 0.7 copy.14
  93.8 1.0 %copy.15 = bf16[128,4096]{1,0:T(8,128)(2,1)} copy(bf16[128,4096]{1,0:T(8,128)(2,1)S(1)} %get-tuple-element.3) | data formatting | bytes 2097152

commit v5 on v0

--- a/solution.py
+++ b/solution.py
@@ -322,6 +322,450 @@
         lax.fori_loop(0, chunks, drain_share, 0)
 
 
+def pair_kernel(
+    n_dp, group, capacity,
+    src_ref, doc_hbm, cos_hbm, sin_hbm, x_hbm, old_hbm, fresh_hbm, k_hbm, v_hbm, g_hbm,
+    out_ref, grad_ref,
+    doc_ref, cos_ref, sin_ref, x_ref, own_ref, g_ref, wkv, wqa, wqb, okv, oqa, oqb, parcel, arrived_0, arrived_1, arrived_2, arrived_3, accq, acckv,
+    dq_ref, dkv_ref, eq_ref, ekv_ref, psend, precv,
+    in_sem, rs, rr, cs, cr, hs, hr, ys, yr, ts, tr, ds, dr, ps, pr,
+):
+    me, head = lax.axis_index("dp"), lax.axis_index("head")
+    rows, hd = k_hbm.shape
+    length = x_ref.shape[0]
+    lanes, ways = 2, 2
+    m = n_dp // lanes
+    half = n_dp // 2
+    core, chip = me % lanes, me // lanes
+    side, level = chip % 2, chip // 2
+    pos = (1 - side) * level + side * (m - 1 - level)
+    piece = rows // ways
+    kv_parts = [(0, first, piece // 4) for first in range(0, piece, piece // 4)]
+    qa_parts = [(1, first, piece // 2) for first in range(0, piece, piece // 2)]
+    qb_parts = [(2, first, piece // 2) for first in range(0, piece, piece // 2)]
+    parts = kv_parts + qa_parts + qb_parts
+    kv_range = range(len(kv_parts))
+    qa_range = range(len(kv_parts), len(kv_parts) + len(qa_parts))
+    qb_range = range(len(kv_parts) + len(qa_parts), len(parts))
+    unit = rows // parcel.shape[0]
+    lead = 3
+    count = m - m // 4
+    signs = (1, -1)
+    arrived = (arrived_0, arrived_1, arrived_2, arrived_3)
+    lag = 1
+    bufs = (wkv, wqa, wqb)
+    others = (okv, oqa, oqb)
+    first_heads = wqa.shape[2] // hd
+    width_a = wqa.shape[2]
+
+    def index_of(p, lane):
+        p = jnp.where(p < 0, p + m, p)
+        p = jnp.where(p >= m, p - m, p)
+        return jnp.where(p < m // 2, 2 * p, 2 * (m - 1 - p) + 1) * lanes + lane
+
+    right, left = index_of(pos + 1, core), index_of(pos - 1, core)
+    targets = (right, left)
+    partner = index_of(pos, 1 - core)
+    across_y = (me, 1 - head)
+
+    loads = [
+        pltpu.make_async_copy(k_hbm, wkv.at[me, :, pl.ds(0, hd)], in_sem.at[0]),
+        pltpu.make_async_copy(v_hbm, wkv.at[me, :, pl.ds(hd, hd)], in_sem.at[1]),
+    ]
+    loads += [
+        pltpu.make_async_copy(old_hbm.at[:, pl.ds(c * hd, hd)], own_ref.at[c], in_sem.at[2 + c])
+        for c in range(group - 1)
+    ]
+    loads += [
+        pltpu.make_async_copy(fresh_hbm, own_ref.at[group - 1], in_sem.at[group + 1]),
+        pltpu.make_async_copy(x_hbm, x_ref, in_sem.at[group + 2]),
+        pltpu.make_async_copy(g_hbm, g_ref, in_sem.at[group + 3]),
+        pltpu.make_async_copy(doc_hbm, doc_ref, in_sem.at[group + 4]),
+        pltpu.make_async_copy(cos_hbm, cos_ref, in_sem.at[group + 5]),
+        pltpu.make_async_copy(sin_hbm, sin_ref, in_sem.at[group + 6]),
+    ]
+    for load in loads:
+        load.start()
+
+    barrier = pltpu.get_barrier_semaphore()
+    peers = [(right, head), (left, head), (partner, head), across_y]
+    for peer in peers:
+        pl.semaphore_signal(barrier, inc=1, device_id=peer, device_id_type=MESH)
+
+    def remote(src, dst, send, recv, device):
+        return pltpu.make_async_remote_copy(
+            src, dst, send, recv, device_id=device, device_id_type=MESH)
+
+    def part_of(p, w, owner):
+        b, first, size = parts[p]
+        return bufs[b].at[owner, pl.ds(w * piece + first, size)]
+
+    def ring(p, w, s, owner):
+        ref = part_of(p, w, owner)
+        return remote(ref, ref, rs.at[parts[p][0]], rr.at[p, s], (targets[w], head))
+
+    def ring_in(p, s):
+        b, _, size = parts[p]
+        ref = bufs[b].at[me, pl.ds(0, ways * size)]
+        return remote(ref, ref, rs.at[b], rr.at[p, s], (left, head))
+
+    def across(p, w, s, owner):
+        ref = part_of(p, w, owner)
+        return remote(ref, ref, cs.at[parts[p][0]], cr.at[parts[p][0], s], (partner, head))
+
+    def across_in(b, s):
+        ref = bufs[b].at[me]
+        return remote(ref, ref, cs.at[b], cr.at[b, s], (partner, head))
+
+    def forward(p, w, owner):
+        b, first, size = parts[p]
+        dst = others[b].at[owner - (1 - head) * half, pl.ds(w * piece + first, size)]
+        return remote(part_of(p, w, owner), dst, ys.at[b], yr.at[b], across_y)
+
+    def owner_at(w, s, lane):
+        return index_of(pos - (1 - 2 * w) * s, lane)
+
+    def share(b, w, s):
+        ref = others[b].at[owner_at(w, s, core) - head * half, pl.ds(pl.multiple_of(w * piece, piece), piece)]
+        return remote(ref, ref, ts.at[b], tr.at[b], (partner, head))
+
+    def all_of(b, count, send, recv):
+        ref = bufs[b].at[pl.ds(0, count), pl.ds(0, piece)]
+        return remote(ref, ref, send.at[b], recv.at[b], across_y)
+
+    def for_here(w, s):
+        return (index_of(pos - signs[w] * s, 0) >= half) == (head == 1)
+
+    def relay(u):
+        return remote(parcel.at[u], arrived[u], hs.at[0], hr.at[u], across_y)
+
+    shift = [(2 - src_ref[k] // group) % 2 for k in range(group)]
+    taken = [src_ref[k] % group for k in range(group)]
+    slot = [
+        sum([(shift[l] == 1).astype(jnp.int32) for l in range(k)], jnp.int32(0)) * shift[k]
+        for k in range(group)
+    ]
+    units = [w * 2 + late for late in range(2) for w in range(ways)]
+
+    for load in loads[:2]:
+        load.wait()
+    pl.semaphore_wait(barrier, len(peers))
+    for p in kv_range:
+        for w in range(ways):
+            ring(p, w, 0, me).start()
+    for p in kv_range:
+        for w in range(ways):
+            across(p, w, 0, me).start()
+    for load in loads[2:2 + group]:
+        load.wait()
+    for c in range(capacity):
+        pick = sum([jnp.where((shift[k] == 1) & (slot[k] == c), taken[k], 0) for k in range(group)], jnp.int32(0))
+        for u in units:
+            parcel[u, c] = own_ref[pick, u * unit:(u + 1) * unit]
+    for u in units:
+        relay(u).start()
+    def by_arrival(to):
+        begin = (2 * to + 3) * (m // 4)
+        places = [(w, lax.rem(signs[w] * (pos - begin - i) + 3 * m, m)) for w in range(ways) for i in range(m // 2)]
+        later = [
+            sum([jnp.where(t > s - (v > w), 1, 0) for v, t in places], jnp.int32(0)) for w, s in places
+        ]
+        order = []
+        for r in range(m):
+            order.append((
+                sum([jnp.where(late == r, w, 0) for late, (w, _) in zip(later, places)], jnp.int32(0)),
+                sum([jnp.where(late == r, s, 0) for late, (_, s) in zip(later, places)], jnp.int32(0)),
+            ))
+        limits = [jnp.int32(-1)] * ways
+        for late, (w, s) in zip(later, places):
+            limits[w] = jnp.maximum(limits[w], jnp.where(late >= m // 4, s, -1))
+        return order, limits
+
+    (order_out, limit_out), (order_in, _) = by_arrival(1 - head), by_arrival(head)
+    far_out, far_in, near_in = order_out[:m // 4], order_in[:m // 4], order_in[m // 4:]
+
+    def forwarded(w, s):
+        return jnp.logical_not(for_here(w, s)) & (s <= limit_out[w])
+
+    def hand_on(some, w, owner, wanted):
+        @pl.when(wanted)
+        def _():
+            for p in some:
+                forward(p, w, owner).start()
+
+    for w in range(ways):
+        hand_on(kv_range, w, me, forwarded(w, 0))
+    for load in loads[2 + group:]:
+        load.wait()
+
+    accs = (acckv, accq.at[:, pl.ds(0, width_a)], accq.at[:, pl.ds(width_a, group * hd - width_a)])
+
+    def add(b, s):
+        across_in(b, s).wait_recv()
+        total = accs[b][...]
+        for lane in range(lanes):
+            for w in range(ways):
+                owner = index_of(pos - signs[w] * s, lane)
+                xs = x_ref[:, pl.ds(pl.multiple_of(owner * rows + w * piece, 128), piece)]
+                total = total + dot(xs, bufs[b][owner, pl.ds(w * piece, piece), :], 1, 0)
+        accs[b][...] = total
+
+    def begin(some, w):
+        for p in some:
+            ring(p, w, 0, me).start()
+        for p in some:
+            across(p, w, 0, me).start()
+        hand_on(some, w, me, forwarded(w, 0))
+
+    def pass_on(some, s):
+        owners = [index_of(pos - signs[w] * s, core) for w in range(ways)]
+        wanted = [forwarded(w, s) for w in range(ways)]
+        for p in some:
+            ring_in(p, s - 1).wait_recv()
+
+            @pl.when(s < m - 1)
+            def _():
+                for w in range(ways):
+                    ring(p, w, s, owners[w]).start()
+
+            for w in range(ways):
+                across(p, w, s, owners[w]).start()
+                hand_on([p], w, owners[w], wanted[w])
+
+    accq[...] = jnp.zeros_like(accq)
+    acckv[...] = jnp.zeros_like(acckv)
+    add(0, 0)
+
+    def assemble(u):
+        relay(u).wait_recv()
+        block = slice(u * unit, (u + 1) * unit)
+        for k in range(group):
+            b, at = (1, k) if k < first_heads else (2, k - first_heads)
+            bufs[b][me, block, at * hd:(at + 1) * hd] = jnp.where(
+                shift[k] == 0, own_ref[taken[k], block], arrived[u][slot[k]])
+        begin([qa_range[u % 2]], u // 2)
+
+    pass_on(kv_range, 1)
+    assemble(units[0])
+    assemble(units[1])
+    pass_on(kv_range, 2)
+    assemble(units[2])
+    assemble(units[3])
+    for w in range(ways):
+        begin(qb_range, w)
+    pass_on(kv_range, 3)
+
+    def step(s, carry):
+        add(0, s)
+
+        @pl.when(s > 0)
+        def _():
+            add(1, s - 1)
+
+        @pl.when(s > lag)
+        def _():
+            add(2, s - 1 - lag)
+
+        @pl.when(s + lead < m)
+        def _():
+            pass_on(kv_range, s + lead)
+
+        @pl.when(s > lag)
+        def _():
+            pass_on(qb_range, s - lag)
+
+        pass_on(qa_range, s)
+        return carry
+
+    lax.fori_loop(1, m, step, 0)
+    add(1, m - 1)
+    for s in range(m - lag, m - 1):
+        add(2, s - 1)
+        pass_on(qb_range, s)
+    scale = 1.0 / math.sqrt(hd)
+    cosine, sine = cos_ref[...], sin_ref[...]
+
+    def rotate(f):
+        return f * cosine + pltpu.roll(f, hd // 2, 1) * sine
+
+    def rotate_back(f):
+        return f * cosine - pltpu.roll(f, hd // 2, 1) * sine
+
+    def swap_q(first, size):
+        cols = pl.ds(first, size)
+        return remote(dq_ref.at[:, cols], eq_ref.at[:, cols], ds.at[0], dr.at[0], across_y)
+
+    swap_kv = remote(dkv_ref, ekv_ref, ds.at[1], dr.at[1], across_y)
+    swap_all_q = remote(dq_ref, eq_ref, ds.at[0], dr.at[0], across_y)
+
+    docs = jnp.broadcast_to(doc_ref[...].astype(jnp.float32), (length, length))
+    at_key = lax.broadcasted_iota(jnp.int32, (length, length), 1)
+    at_query = lax.broadcasted_iota(jnp.int32, (length, length), 0)
+    allowed = (at_key <= at_query) & (docs == docs.T)
+    key = rotate(acckv[:, :hd]).astype(jnp.bfloat16)
+    value = acckv[:, hd:].astype(jnp.bfloat16)
+
+    def attend(heads):
+        cols = [slice(k * hd, (k + 1) * hd) for k in heads]
+        block = [slice(i * length, (i + 1) * length) for i in range(len(heads))]
+        query = jnp.concatenate([rotate(accq[:, c]).astype(jnp.bfloat16) for c in cols], axis=0)
+        given = jnp.concatenate([g_ref[:, c] for c in cols], axis=0)
+        mask = jnp.concatenate([allowed] * len(heads), axis=0)
+        scores = jnp.where(mask, dot(query, key, 1, 1) * scale, neg_large)
+        weights = jnp.exp(scores - jnp.max(scores, axis=-1, keepdims=True))
+        probs = weights / jnp.sum(weights, axis=-1, keepdims=True)
+        probs_b = probs.astype(jnp.bfloat16)
+        prob_grad = dot(given, value, 1, 1)
+        centre = jnp.sum(probs * prob_grad, axis=-1, keepdims=True)
+        dscore = (probs * (prob_grad - centre) * scale).astype(jnp.bfloat16)
+        dquery = dot(dscore, key, 1, 0)
+        for c, r in zip(cols, block):
+            dq_ref[:, c] = rotate_back(dquery[r]).astype(jnp.bfloat16)
+        swap_q(heads[0] * hd, len(heads) * hd).start()
+        attended = dot(probs_b, value, 1, 0).astype(jnp.bfloat16)
+        for c, r in zip(cols, block):
+            out_ref[:, c] = attended[r]
+        return dot(dscore, query, 0, 0), dot(probs_b, given, 0, 0)
+
+    dkey, dvalue = attend(range(first_heads))
+    add(2, m - 2)
+    pass_on(qb_range, m - 1)
+    add(2, m - 1)
+    late_dkey, late_dvalue = attend(range(first_heads, group))
+    dkey, dvalue = dkey + late_dkey, dvalue + late_dvalue
+    dkv_ref[:, :hd] = rotate_back(dkey).astype(jnp.bfloat16)
+    dkv_ref[:, hd:] = dvalue.astype(jnp.bfloat16)
+    swap_kv.start()
+
+    def partial(dq, dkv, weights, place, w):
+        block = pl.ds(pl.multiple_of(w * piece, piece), piece)
+        wk, wa, wb = weights
+        return (dot(dq[:, :width_a], wa[place, block, :], 1, 1)
+                + dot(dq[:, width_a:], wb[place, block, :], 1, 1)
+                + dot(dkv[...], wk[place, block, :], 1, 1)).astype(jnp.bfloat16)
+
+    def send_share(r, lane):
+        return remote(psend.at[r, lane], precv.at[r, lane], ps.at[0], pr.at[r, lane], across_y)
+
+    for r, (w, s) in enumerate(far_out):
+        for lane in range(lanes):
+            psend[r, lane] = partial(dq_ref, dkv_ref, bufs, owner_at(w, s, lane), w)
+            send_share(r, lane).start()
+
+    for b in range(3):
+        all_of(b, count, ys, yr).wait_recv()
+    for w, s in near_in:
+        for b in range(3):
+            share(b, w, s).start()
+
+    def columns(place, w):
+        return pl.ds(pl.multiple_of(place * rows + w * piece, piece), piece)
+
+    def own_part(i, carry):
+        for place in (2 * i, 2 * i + 1):
+            for w in range(ways):
+                grad_ref[:, columns(place, w)] = partial(dq_ref, dkv_ref, bufs, head * half + place, w)
+        return carry
+
+    lax.fori_loop(0, half // 2, own_part, 0)
+    swap_all_q.wait_recv()
+    swap_kv.wait_recv()
+    for b in range(3):
+        all_of(b, count, ts, tr).wait_recv()
+
+    def plus(place, w, value):
+        cols = columns(place, w)
+        grad_ref[:, cols] = (grad_ref[:, cols].astype(jnp.float32) + value.astype(jnp.float32)).astype(jnp.bfloat16)
+
+    for w, s in near_in:
+        for lane in range(lanes):
+            place = owner_at(w, s, lane) - head * half
+            plus(place, w, partial(eq_ref, ekv_ref, others, place, w))
+    for r, (w, s) in enumerate(far_in):
+        for lane in range(lanes):
+            send_share(r, lane).wait_recv()
+            plus(owner_at(w, s, lane) - head * half, w, precv[r, lane])
+
+    for b in range(3):
+        for number, sent in ((ways * (m - 1), rs), (ways * m, cs), (count, ys), (count, ts)):
+            all_of(b, number, sent, sent).wait_send()
+    remote(parcel, parcel, hs.at[0], hr.at[0], across_y).wait_send()
+    swap_all_q.wait_send()
+    swap_kv.wait_send()
+    remote(psend, psend, ps.at[0], ps.at[0], across_y).wait_send()
+
+
+def pair_call(n_dp, x, old, fresh, wk, wv, g, head_source, doc_ids):
+    length, width = x.shape
+    rows, hd = wk.shape
+    group = g.shape[1] // hd
+    m, half, ways, units, parts = n_dp // 2, n_dp // 2, 2, 4, 8
+    late = 2 * hd
+    early = group * hd - late
+    capacity = (group + 1) // 2
+    cosine, sine = rotary_tables(length, hd)
+    bf, f32 = jnp.bfloat16, jnp.float32
+    vm = pl.BlockSpec(memory_space=pltpu.VMEM)
+    anyspace = pl.BlockSpec(memory_space=pl.ANY)
+    dma = pltpu.SemaphoreType.DMA
+    unit = rows // units
+    far = (m // 4, 2)
+    return pl.pallas_call(
+        functools.partial(pair_kernel, n_dp, group, capacity),
+        out_shape=(
+            pltpu.VMEM((length, group * hd), bf),
+            pltpu.VMEM((length, width // 2), bf),
+        ),
+        in_specs=[pl.BlockSpec(memory_space=pltpu.SMEM)] + [anyspace] * 9,
+        out_specs=(vm, vm),
+        scratch_shapes=[
+            pltpu.VMEM((1, length), jnp.int32),
+            pltpu.VMEM((length, hd), f32),
+            pltpu.VMEM((length, hd), f32),
+            pltpu.VMEM((length, width), bf),
+            pltpu.VMEM((group, rows, hd), bf),
+            pltpu.VMEM((length, group * hd), bf),
+            pltpu.VMEM((n_dp, rows, 2 * hd), bf),
+            pltpu.VMEM((n_dp, rows, early), bf),
+            pltpu.VMEM((n_dp, rows, late), bf),
+            pltpu.VMEM((half, rows, 2 * hd), bf),
+            pltpu.VMEM((half, rows, early), bf),
+            pltpu.VMEM((half, rows, late), bf),
+            pltpu.VMEM((units, capacity, unit, hd), bf),
+            pltpu.VMEM((capacity, unit, hd), bf),
+            pltpu.VMEM((capacity, unit, hd), bf),
+            pltpu.VMEM((capacity, unit, hd), bf),
+            pltpu.VMEM((capacity, unit, hd), bf),
+            pltpu.VMEM((length, group * hd), f32),
+            pltpu.VMEM((length, 2 * hd), f32),
+            pltpu.VMEM((length, group * hd), bf),
+            pltpu.VMEM((length, 2 * hd), bf),
+            pltpu.VMEM((length, group * hd), bf),
+            pltpu.VMEM((length, 2 * hd), bf),
+            pltpu.VMEM(far + (length, rows // ways), bf),
+            pltpu.VMEM(far + (length, rows // ways), bf),
+            dma((group + 7,)),
+            dma((3,)),
+            dma((parts, m)),
+            dma((3,)),
+            dma((3, m)),
+            dma((1,)),
+            dma((units,)),
+            dma((3,)),
+            dma((3,)),
+            dma((3,)),
+            dma((3,)),
+            dma((2,)),
+            dma((2,)),
+            dma((1,)),
+            dma(far),
+        ],
+        compiler_params=pltpu.CompilerParams(
+            collective_id=0, has_side_effects=True, vmem_limit_bytes=48*1024*1024),
+    )(*(pltpu.with_memory_space_constraint(jnp.asarray(a), pltpu.HBM) for a in (
+        head_source, doc_ids.reshape(1, -1), cosine, sine, x, old, fresh, wk, wv, g)))
+
+
 def solution(mesh):
     n_dp, n_head = mesh.shape["dp"], mesh.shape["head"]
 
@@ -331,6 +775,8 @@
         group = g.shape[1] // hd
         ways = 2 if rows % 256 == 0 else 1
         m = n_dp // 2
+        if n_head == 2 and group > 2 and rows % 512 == 0 and m % 8 == 0:
+            return pair_call(n_dp, x, old, fresh, wk, wv, g, head_source, doc_ids)
         capacity = (group + n_head - 1) // n_head
         chunks = n_dp // n_head
         cosine, sine = rotary_tables(length, hd)

time: 116 us -> 91.9 us (0.79)
  Pallas kernels: 111 us -> 89.4 us
  local copies, waits for them, and re-layouts: 3.88 us -> 1.64 us
    pallas_call x1, Pallas kernels: 111 us -> 89.4 us  [pair_call(): pl.pallas_call(functools.partial(pair_kernel, n_dp, group, capacity), out...]
    unnamed x2, local copies, waits for them, and re-layouts: 3.88 us -> 1.64 us
where the time goes in v5:
time: 91.9 us; the launch traced here: 91.7 us
  Pallas kernels  89.4 us (97%)
  local copies, waits for them, and re-layouts  1.64 us (2%)
    pallas_call x1, Pallas kernels, pair_call(): pl.pallas_call(functools.partial(pair_kernel, n_dp, group, capacity), out...  89.4 us

profile of v5, /device:TPU:0, one launch (start us, length us, event | category | flops | bytes accessed | tf_op | source)
XLA Modules:
  0.0 91.7 jit_solution(991691232721688219)
XLA Ops:
  0.6 89.4 %shard_map.113 = (bf16[128,640]{1,0:T(8,128)(2,1)S(1)}, bf16[128,4096]{1,0:T(8,128)(2,1)S(1)}) custom-call(s32[10]{0:T(128)} %src_ref.1, s32[1,128]{1,0:T(1,128)} %bitcast.1, f32[128,128]{1,0:T(8,128)} %constant.4.clone.cos_hbm, f32[128,128]{1,0:T(8,128)} %constant.5.clone.sin_hbm, bf16[128,8192]{1,0:T(8,128)(2,1)} %x_hbm.1, bf16[512,512]{1,0:T(8,128)(2,1)} %old_hbm.1, ...), custom_call_target="tpu_custom_call" | custom-call | tf_op jit(solution)/shard_map/pallas_call | solution.py:713
  90.1 0.7 copy.14
  90.7 1.0 %copy.15 = bf16[128,4096]{1,0:T(8,128)(2,1)} copy(bf16[128,4096]{1,0:T(8,128)(2,1)S(1)} %get-tuple-element.3) | data formatting | bytes 2097152

commit v6 on v5

--- a/solution.py
+++ b/solution.py
@@ -324,9 +324,9 @@
 
 def pair_kernel(
     n_dp, group, capacity,
-    src_ref, doc_hbm, cos_hbm, sin_hbm, x_hbm, old_hbm, fresh_hbm, k_hbm, v_hbm, g_hbm,
+    src_hbm, doc_hbm, cos_hbm, sin_hbm, x_hbm, old_hbm, fresh_hbm, k_hbm, v_hbm, g_hbm,
     out_ref, grad_ref,
-    doc_ref, cos_ref, sin_ref, x_ref, own_ref, g_ref, wkv, wqa, wqb, okv, oqa, oqb, parcel, arrived_0, arrived_1, arrived_2, arrived_3, accq, acckv,
+    src_ref, doc_ref, cos_ref, sin_ref, x_ref, own_ref, g_ref, wkv, wqa, wqb, okv, oqa, oqb, parcel, arrived_0, arrived_1, arrived_2, arrived_3, accq, acckv,
     dq_ref, dkv_ref, eq_ref, ekv_ref, psend, precv,
     in_sem, rs, rr, cs, cr, hs, hr, ys, yr, ts, tr, ds, dr, ps, pr,
 ):
@@ -340,9 +340,9 @@
     side, level = chip % 2, chip // 2
     pos = (1 - side) * level + side * (m - 1 - level)
     piece = rows // ways
-    kv_parts = [(0, first, piece // 4) for first in range(0, piece, piece // 4)]
+    kv_parts = [(0, first, piece // 2) for first in range(0, piece, piece // 2)]
     qa_parts = [(1, first, piece // 2) for first in range(0, piece, piece // 2)]
-    qb_parts = [(2, first, piece // 2) for first in range(0, piece, piece // 2)]
+    qb_parts = [(2, first, piece // 1) for first in range(0, piece, piece // 1)]
     parts = kv_parts + qa_parts + qb_parts
     kv_range = range(len(kv_parts))
     qa_range = range(len(kv_parts), len(kv_parts) + len(qa_parts))
@@ -352,7 +352,6 @@
     count = m - m // 4
     signs = (1, -1)
     arrived = (arrived_0, arrived_1, arrived_2, arrived_3)
-    lag = 1
     bufs = (wkv, wqa, wqb)
     others = (okv, oqa, oqb)
     first_heads = wqa.shape[2] // hd
@@ -367,6 +366,11 @@
     targets = (right, left)
     partner = index_of(pos, 1 - core)
     across_y = (me, 1 - head)
+
+    barrier = pltpu.get_barrier_semaphore()
+    peers = [(right, head), (left, head), (partner, head), across_y]
+    for peer in peers:
+        pl.semaphore_signal(barrier, inc=1, device_id=peer, device_id_type=MESH)
 
     loads = [
         pltpu.make_async_copy(k_hbm, wkv.at[me, :, pl.ds(0, hd)], in_sem.at[0]),
@@ -378,6 +382,7 @@
     ]
     loads += [
         pltpu.make_async_copy(fresh_hbm, own_ref.at[group - 1], in_sem.at[group + 1]),
+        pltpu.make_async_copy(src_hbm, src_ref, in_sem.at[group + 7]),
         pltpu.make_async_copy(x_hbm, x_ref, in_sem.at[group + 2]),
         pltpu.make_async_copy(g_hbm, g_ref, in_sem.at[group + 3]),
         pltpu.make_async_copy(doc_hbm, doc_ref, in_sem.at[group + 4]),
@@ -387,11 +392,6 @@
     for load in loads:
         load.start()
 
-    barrier = pltpu.get_barrier_semaphore()
-    peers = [(right, head), (left, head), (partner, head), across_y]
-    for peer in peers:
-        pl.semaphore_signal(barrier, inc=1, device_id=peer, device_id_type=MESH)
-
     def remote(src, dst, send, recv, device):
         return pltpu.make_async_remote_copy(
             src, dst, send, recv, device_id=device, device_id_type=MESH)
@@ -439,12 +439,6 @@
     def relay(u):
         return remote(parcel.at[u], arrived[u], hs.at[0], hr.at[u], across_y)
 
-    shift = [(2 - src_ref[k] // group) % 2 for k in range(group)]
-    taken = [src_ref[k] % group for k in range(group)]
-    slot = [
-        sum([(shift[l] == 1).astype(jnp.int32) for l in range(k)], jnp.int32(0)) * shift[k]
-        for k in range(group)
-    ]
     units = [w * 2 + late for late in range(2) for w in range(ways)]
 
     for load in loads[:2]:
@@ -456,14 +450,23 @@
     for p in kv_range:
         for w in range(ways):
             across(p, w, 0, me).start()
-    for load in loads[2:2 + group]:
+    for load in loads[2:3 + group]:
         load.wait()
-    for c in range(capacity):
-        pick = sum([jnp.where((shift[k] == 1) & (slot[k] == c), taken[k], 0) for k in range(group)], jnp.int32(0))
-        for u in units:
-            parcel[u, c] = own_ref[pick, u * unit:(u + 1) * unit]
+    shift = [(2 - src_ref[0, k] // group) % 2 for k in range(group)]
+    taken = [src_ref[0, k] % group for k in range(group)]
+    slot = [
+        sum([(shift[l] == 1).astype(jnp.int32) for l in range(k)], jnp.int32(0)) * shift[k]
+        for k in range(group)
+    ]
+    picks = [
+        sum([jnp.where((shift[k] == 1) & (slot[k] == c), taken[k], 0) for k in range(group)], jnp.int32(0))
+        for c in range(capacity)
+    ]
     for u in units:
+        for c in range(capacity):
+            parcel[u, c] = own_ref[picks[c], u * unit:(u + 1) * unit]
         relay(u).start()
+
     def by_arrival(to):
         begin = (2 * to + 3) * (m // 4)
         places = [(w, lax.rem(signs[w] * (pos - begin - i) + 3 * m, m)) for w in range(ways) for i in range(m // 2)]
@@ -495,20 +498,23 @@
 
     for w in range(ways):
         hand_on(kv_range, w, me, forwarded(w, 0))
-    for load in loads[2 + group:]:
+    for load in loads[3 + group:]:
         load.wait()
 
     accs = (acckv, accq.at[:, pl.ds(0, width_a)], accq.at[:, pl.ds(width_a, group * hd - width_a)])
 
-    def add(b, s):
-        across_in(b, s).wait_recv()
+    def add_lanes(b, s, some):
         total = accs[b][...]
-        for lane in range(lanes):
+        for lane in some:
             for w in range(ways):
                 owner = index_of(pos - signs[w] * s, lane)
                 xs = x_ref[:, pl.ds(pl.multiple_of(owner * rows + w * piece, 128), piece)]
                 total = total + dot(xs, bufs[b][owner, pl.ds(w * piece, piece), :], 1, 0)
         accs[b][...] = total
+
+    def add(b, s):
+        across_in(b, s).wait_recv()
+        add_lanes(b, s, range(lanes))
 
     def begin(some, w):
         for p in some:
@@ -562,26 +568,26 @@
         def _():
             add(1, s - 1)
 
-        @pl.when(s > lag)
+        @pl.when(s > 1)
         def _():
-            add(2, s - 1 - lag)
+            add(2, s - 2)
 
         @pl.when(s + lead < m)
         def _():
             pass_on(kv_range, s + lead)
 
-        @pl.when(s > lag)
+        @pl.when(s > 1)
         def _():
-            pass_on(qb_range, s - lag)
+            pass_on(qb_range, s - 1)
 
         pass_on(qa_range, s)
         return carry
 
     lax.fori_loop(1, m, step, 0)
-    add(1, m - 1)
-    for s in range(m - lag, m - 1):
-        add(2, s - 1)
-        pass_on(qb_range, s)
+    add(2, m - 2)
+    add_lanes(1, m - 1, [core])
+    across_in(1, m - 1).wait_recv()
+    add_lanes(1, m - 1, [1 - core])
     scale = 1.0 / math.sqrt(hd)
     cosine, sine = cos_ref[...], sin_ref[...]
 
@@ -628,9 +634,10 @@
         return dot(dscore, query, 0, 0), dot(probs_b, given, 0, 0)
 
     dkey, dvalue = attend(range(first_heads))
-    add(2, m - 2)
     pass_on(qb_range, m - 1)
-    add(2, m - 1)
+    add_lanes(2, m - 1, [core])
+    across_in(2, m - 1).wait_recv()
+    add_lanes(2, m - 1, [1 - core])
     late_dkey, late_dvalue = attend(range(first_heads, group))
     dkey, dvalue = dkey + late_dkey, dvalue + late_dvalue
     dkv_ref[:, :hd] = rotate_back(dkey).astype(jnp.bfloat16)
@@ -695,11 +702,22 @@
     remote(psend, psend, ps.at[0], ps.at[0], across_y).wait_send()
 
 
+def put_out(attended_ref, grad_ref, out_hbm, grad_hbm, sem):
+    copies = [
+        pltpu.make_async_copy(attended_ref, out_hbm, sem.at[0]),
+        pltpu.make_async_copy(grad_ref, grad_hbm, sem.at[1]),
+    ]
+    for copy in copies:
+        copy.start()
+    for copy in copies:
+        copy.wait()
+
+
 def pair_call(n_dp, x, old, fresh, wk, wv, g, head_source, doc_ids):
     length, width = x.shape
     rows, hd = wk.shape
     group = g.shape[1] // hd
-    m, half, ways, units, parts = n_dp // 2, n_dp // 2, 2, 4, 8
+    m, half, ways, units, parts = n_dp // 2, n_dp // 2, 2, 4, 5
     late = 2 * hd
     early = group * hd - late
     capacity = (group + 1) // 2
@@ -710,15 +728,16 @@
     dma = pltpu.SemaphoreType.DMA
     unit = rows // units
     far = (m // 4, 2)
-    return pl.pallas_call(
+    attended, grad = pl.pallas_call(
         functools.partial(pair_kernel, n_dp, group, capacity),
         out_shape=(
             pltpu.VMEM((length, group * hd), bf),
             pltpu.VMEM((length, width // 2), bf),
         ),
-        in_specs=[pl.BlockSpec(memory_space=pltpu.SMEM)] + [anyspace] * 9,
+        in_specs=[anyspace] * 10,
         out_specs=(vm, vm),
         scratch_shapes=[
+            pltpu.SMEM((1, head_source.shape[0]), jnp.int32),
             pltpu.VMEM((1, length), jnp.int32),
             pltpu.VMEM((length, hd), f32),
             pltpu.VMEM((length, hd), f32),
@@ -744,7 +763,7 @@
             pltpu.VMEM((length, 2 * hd), bf),
             pltpu.VMEM(far + (length, rows // ways), bf),
             pltpu.VMEM(far + (length, rows // ways), bf),
-            dma((group + 7,)),
+            dma((group + 8,)),
             dma((3,)),
             dma((parts, m)),
             dma((3,)),
@@ -763,7 +782,15 @@
         compiler_params=pltpu.CompilerParams(
             collective_id=0, has_side_effects=True, vmem_limit_bytes=48*1024*1024),
     )(*(pltpu.with_memory_space_constraint(jnp.asarray(a), pltpu.HBM) for a in (
-        head_source, doc_ids.reshape(1, -1), cosine, sine, x, old, fresh, wk, wv, g)))
+        head_source.reshape(1, -1), doc_ids.reshape(1, -1), cosine, sine, x, old, fresh, wk, wv, g)))
+    return pl.pallas_call(
+        put_out,
+        out_shape=(pltpu.HBM(attended.shape, bf), pltpu.HBM(grad.shape, bf)),
+        in_specs=[vm, vm],
+        out_specs=(anyspace, anyspace),
+        scratch_shapes=[dma((2,))],
+        compiler_params=pltpu.CompilerParams(vmem_limit_bytes=1024 * 1024),
+    )(pltpu.with_memory_space_constraint(attended, pltpu.VMEM), pltpu.with_memory_space_constraint(grad, pltpu.VMEM))
 
 
 def solution(mesh):

time: 91.9 us -> 90.7 us (0.987)
  local copies, waits for them, and re-layouts: 1.64 us -> 0 us
    unnamed x2 -> x0, local copies, waits for them, and re-layouts: 1.64 us -> none
    pallas_call x0 -> x1, Pallas kernels: none -> 1.04 us  [pair_call(): pl.pallas_call(put_out, out_shape=(pltpu.HBM(attended.shape, bf), pltpu.H...]
where the time goes in v6:
time: 90.7 us; the launch traced here: 90.6 us
  Pallas kernels  89.9 us (99%)
    pallas_call x1, Pallas kernels, pair_call(): pl.pallas_call(functools.partial(pair_kernel, n_dp, group, capacity), out...  88.9 us

profile of v6, /device:TPU:0, one launch (start us, length us, event | category | flops | bytes accessed | tf_op | source)
XLA Modules:
  0.0 90.6 jit_solution(13156239454933502992)
XLA Ops:
  0.6 88.9 %shard_map.113 = (bf16[128,640]{1,0:T(8,128)(2,1)S(1)}, bf16[128,4096]{1,0:T(8,128)(2,1)S(1)}) custom-call(s32[1,10]{1,0:T(1,128)} %bitcast.2, s32[1,128]{1,0:T(1,128)} %bitcast.3, f32[128,128]{1,0:T(8,128)} %constant.4.clone.cos_hbm, f32[128,128]{1,0:T(8,128)} %constant.5.clone.sin_hbm, bf16[128,8192]{1,0:T(8,128)(2,1)} %x_hbm.1, bf16[512,512]{1,0:T(8,128)(2,1)} %old_hbm.1, ...), custom_call_target="tpu_custom_call" | custom-call | tf_op jit(solution)/shard_map/pallas_call | solution.py:731
  89.5 1.0 %shard_map.114 = (bf16[128,640]{1,0:T(8,128)(2,1)}, bf16[128,4096]{1,0:T(8,128)(2,1)}) custom-call(bf16[128,640]{1,0:T(8,128)(2,1)S(1)} %get-tuple-element.4.attended_ref, bf16[128,4096]{1,0:T(8,128)(2,1)S(1)} %get-tuple-element.5.grad_ref), custom_call_target="tpu_custom_call" | custom-call | tf_op jit(solution)/shard_map/pallas_call | solution.py:786

commit v7 on v6

--- a/solution.py
+++ b/solution.py
@@ -586,8 +586,6 @@
     lax.fori_loop(1, m, step, 0)
     add(2, m - 2)
     add_lanes(1, m - 1, [core])
-    across_in(1, m - 1).wait_recv()
-    add_lanes(1, m - 1, [1 - core])
     scale = 1.0 / math.sqrt(hd)
     cosine, sine = cos_ref[...], sin_ref[...]
 
@@ -611,17 +609,19 @@
     key = rotate(acckv[:, :hd]).astype(jnp.bfloat16)
     value = acckv[:, hd:].astype(jnp.bfloat16)
 
-    def attend(heads):
+    def prepare(heads):
+        given = jnp.concatenate([g_ref[:, k * hd:(k + 1) * hd] for k in heads], axis=0)
+        return given, dot(given, value, 1, 1)
+
+    def attend(heads, given, prob_grad):
         cols = [slice(k * hd, (k + 1) * hd) for k in heads]
         block = [slice(i * length, (i + 1) * length) for i in range(len(heads))]
         query = jnp.concatenate([rotate(accq[:, c]).astype(jnp.bfloat16) for c in cols], axis=0)
-        given = jnp.concatenate([g_ref[:, c] for c in cols], axis=0)
         mask = jnp.concatenate([allowed] * len(heads), axis=0)
         scores = jnp.where(mask, dot(query, key, 1, 1) * scale, neg_large)
         weights = jnp.exp(scores - jnp.max(scores, axis=-1, keepdims=True))
         probs = weights / jnp.sum(weights, axis=-1, keepdims=True)
         probs_b = probs.astype(jnp.bfloat16)
-        prob_grad = dot(given, value, 1, 1)
         centre = jnp.sum(probs * prob_grad, axis=-1, keepdims=True)
         dscore = (probs * (prob_grad - centre) * scale).astype(jnp.bfloat16)
         dquery = dot(dscore, key, 1, 0)
@@ -633,12 +633,15 @@
             out_ref[:, c] = attended[r]
         return dot(dscore, query, 0, 0), dot(probs_b, given, 0, 0)
 
-    dkey, dvalue = attend(range(first_heads))
+    early, late = prepare(range(first_heads)), prepare(range(first_heads, group))
+    across_in(1, m - 1).wait_recv()
+    add_lanes(1, m - 1, [1 - core])
+    dkey, dvalue = attend(range(first_heads), *early)
     pass_on(qb_range, m - 1)
     add_lanes(2, m - 1, [core])
     across_in(2, m - 1).wait_recv()
     add_lanes(2, m - 1, [1 - core])
-    late_dkey, late_dvalue = attend(range(first_heads, group))
+    late_dkey, late_dvalue = attend(range(first_heads, group), *late)
     dkey, dvalue = dkey + late_dkey, dvalue + late_dvalue
     dkv_ref[:, :hd] = rotate_back(dkey).astype(jnp.bfloat16)
     dkv_ref[:, hd:] = dvalue.astype(jnp.bfloat16)

time: 90.7 us -> 90.8 us (level)
  no operation moved by 1% of the time
where the time goes in v7:
time: 90.8 us; the launch traced here: 90.7 us
  Pallas kernels  90 us (99%)
    pallas_call x1, Pallas kernels, pair_call(): pl.pallas_call(functools.partial(pair_kernel, n_dp, group, capacity), out...  89 us

profile of v7, /device:TPU:0, one launch (start us, length us, event | category | flops | bytes accessed | tf_op | source)
XLA Modules:
  0.0 90.7 jit_solution(1199567893702188395)
XLA Ops:
  0.6 89.0 %shard_map.113 = (bf16[128,640]{1,0:T(8,128)(2,1)S(1)}, bf16[128,4096]{1,0:T(8,128)(2,1)S(1)}) custom-call(s32[1,10]{1,0:T(1,128)} %bitcast.2, s32[1,128]{1,0:T(1,128)} %bitcast.3, f32[128,128]{1,0:T(8,128)} %constant.4.clone.cos_hbm, f32[128,128]{1,0:T(8,128)} %constant.5.clone.sin_hbm, bf16[128,8192]{1,0:T(8,128)(2,1)} %x_hbm.1, bf16[512,512]{1,0:T(8,128)(2,1)} %old_hbm.1, ...), custom_call_target="tpu_custom_call" | custom-call | tf_op jit(solution)/shard_map/pallas_call | solution.py:734
  89.6 1.0 %shard_map.114 = (bf16[128,640]{1,0:T(8,128)(2,1)}, bf16[128,4096]{1,0:T(8,128)(2,1)}) custom-call(bf16[128,640]{1,0:T(8,128)(2,1)S(1)} %get-tuple-element.4.attended_ref, bf16[128,4096]{1,0:T(8,128)(2,1)S(1)} %get-tuple-element.5.grad_ref), custom_call_target="tpu_custom_call" | custom-call | tf_op jit(solution)/shard_map/pallas_call | solution.py:789

commit v8 on v7

--- a/solution.py
+++ b/solution.py
@@ -600,6 +600,11 @@
         return remote(dq_ref.at[:, cols], eq_ref.at[:, cols], ds.at[0], dr.at[0], across_y)
 
     swap_kv = remote(dkv_ref, ekv_ref, ds.at[1], dr.at[1], across_y)
+
+    def swap_part(first):
+        cols = pl.ds(first, hd)
+        return remote(dkv_ref.at[:, cols], ekv_ref.at[:, cols], ds.at[1], dr.at[1], across_y)
+
     swap_all_q = remote(dq_ref, eq_ref, ds.at[0], dr.at[0], across_y)
 
     docs = jnp.broadcast_to(doc_ref[...].astype(jnp.float32), (length, length))
@@ -613,7 +618,7 @@
         given = jnp.concatenate([g_ref[:, k * hd:(k + 1) * hd] for k in heads], axis=0)
         return given, dot(given, value, 1, 1)
 
-    def attend(heads, given, prob_grad):
+    def attend(heads, given, prob_grad, before=None):
         cols = [slice(k * hd, (k + 1) * hd) for k in heads]
         block = [slice(i * length, (i + 1) * length) for i in range(len(heads))]
         query = jnp.concatenate([rotate(accq[:, c]).astype(jnp.bfloat16) for c in cols], axis=0)
@@ -622,6 +627,10 @@
         weights = jnp.exp(scores - jnp.max(scores, axis=-1, keepdims=True))
         probs = weights / jnp.sum(weights, axis=-1, keepdims=True)
         probs_b = probs.astype(jnp.bfloat16)
+        dvalue = dot(probs_b, given, 0, 0)
+        if before is not None:
+            dkv_ref[:, hd:] = (before + dvalue).astype(jnp.bfloat16)
+            swap_part(hd).start()
         centre = jnp.sum(probs * prob_grad, axis=-1, keepdims=True)
         dscore = (probs * (prob_grad - centre) * scale).astype(jnp.bfloat16)
         dquery = dot(dscore, key, 1, 0)
@@ -631,7 +640,7 @@
         attended = dot(probs_b, value, 1, 0).astype(jnp.bfloat16)
         for c, r in zip(cols, block):
             out_ref[:, c] = attended[r]
-        return dot(dscore, query, 0, 0), dot(probs_b, given, 0, 0)
+        return dot(dscore, query, 0, 0), dvalue
 
     early, late = prepare(range(first_heads)), prepare(range(first_heads, group))
     across_in(1, m - 1).wait_recv()
@@ -641,11 +650,10 @@
     add_lanes(2, m - 1, [core])
     across_in(2, m - 1).wait_recv()
     add_lanes(2, m - 1, [1 - core])
-    late_dkey, late_dvalue = attend(range(first_heads, group), *late)
-    dkey, dvalue = dkey + late_dkey, dvalue + late_dvalue
+    late_dkey, _ = attend(range(first_heads, group), *late, before=dvalue)
+    dkey = dkey + late_dkey
     dkv_ref[:, :hd] = rotate_back(dkey).astype(jnp.bfloat16)
-    dkv_ref[:, hd:] = dvalue.astype(jnp.bfloat16)
-    swap_kv.start()
+    swap_part(0).start()
 
     def partial(dq, dkv, weights, place, w):
         block = pl.ds(pl.multiple_of(w * piece, piece), piece)

time: 90.8 us -> 90.8 us (level)
  no operation moved by 1% of the time
where the time goes in v8:
time: 90.8 us; the launch traced here: 90.7 us
  Pallas kernels  90 us (99%)
    pallas_call x1, Pallas kernels, pair_call(): pl.pallas_call(functools.partial(pair_kernel, n_dp, group, capacity), out...  89 us

profile of v8, /device:TPU:0, one launch (start us, length us, event | category | flops | bytes accessed | tf_op | source)
XLA Modules:
  0.0 90.7 jit_solution(12722867939533203850)
XLA Ops:
  0.6 89.0 %shard_map.113 = (bf16[128,640]{1,0:T(8,128)(2,1)S(1)}, bf16[128,4096]{1,0:T(8,128)(2,1)S(1)}) custom-call(s32[1,10]{1,0:T(1,128)} %bitcast.2, s32[1,128]{1,0:T(1,128)} %bitcast.3, f32[128,128]{1,0:T(8,128)} %constant.4.clone.cos_hbm, f32[128,128]{1,0:T(8,128)} %constant.5.clone.sin_hbm, bf16[128,8192]{1,0:T(8,128)(2,1)} %x_hbm.1, bf16[512,512]{1,0:T(8,128)(2,1)} %old_hbm.1, ...), custom_call_target="tpu_custom_call" | custom-call | tf_op jit(solution)/shard_map/pallas_call | solution.py:742
  89.6 1.0 %shard_map.114 = (bf16[128,640]{1,0:T(8,128)(2,1)}, bf16[128,4096]{1,0:T(8,128)(2,1)}) custom-call(bf16[128,640]{1,0:T(8,128)(2,1)S(1)} %get-tuple-element.4.attended_ref, bf16[128,4096]{1,0:T(8,128)(2,1)S(1)} %get-tuple-element.5.grad_ref), custom_call_target="tpu_custom_call" | custom-call | tf_op jit(solution)/shard_map/pallas_call | solution.py:797
